TPU v7x, 32 devices: a whole 2x2x4 slice. The times are simulated.
32 devices in a mesh: tm: 4 (over z), lat: 8 (over y, x, core).
Axes of the slice: x: 2, y: 2, z: 4, core: 2. Of those that a mesh axis runs over, the one named last changes fastest.
Arguments:
- frames: bfloat16 [256, 512, 1024], P('tm', 'lat'), may hold values from -6 to 6
- projection: bfloat16 [256, 512, 256], P(('tm', 'lat')), may hold values from -0.25 to 0.25
- degree_range: int32 [256, 2], replicated, may hold values from 0 to 256, as said below
- offsets: int32 [8], replicated, may hold values from 0 to 63
Outputs:
- coupling: bfloat16 [256, 2, 8, 256, 2, 256], P(('tm', 'lat'))
Inputs may be any that keep to these rules, and one draw needn't show every extreme that they name: `degree_range`: row m holds lo and hi with min(m, 255) <= lo < hi <= 256.
All inputs are finite; a program needn't handle non-finite values.
Results may differ from a plain program's by a relative error of at most 0.0093.
Values may be sent and summed in bfloat16 or wider, within the bound.
No kernel may reach another device: no remote copies, remote signals or barrier semaphores. Data moves between devices by JAX's collectives and lax.ppermute only.
A program may use at most 192 MiB of HBM per device.

v0:
```python
import math

import jax
import jax.numpy as jnp
from jax import lax
from jax.sharding import PartitionSpec as P


def shifted_2(block, axis, distance):
    devices = range(lax.axis_size(axis))
    route = [(i - distance, i) for i in devices if i - distance in devices]
    return lax.ppermute(block, axis, route)


def longitude_table(lon_count, order_ids):
    longitude_points = jnp.arange(lon_count, dtype=jnp.int32)
    rotation_radians = longitude_points[:, None] * order_ids[None, :] % lon_count
    angle = rotation_radians.astype(jnp.float32) * (2.0 * math.pi / lon_count)
    factor = 1.0 / math.sqrt(lon_count)
    table = jnp.stack([jnp.cos(angle) * factor, -jnp.sin(angle) * factor], axis=2)
    return table.reshape(lon_count, -1).astype(jnp.bfloat16)


def time_table(entry_total):
    observation_epochs = jnp.arange(entry_total, dtype=jnp.int32)
    rotation_radians = observation_epochs[:, None] * observation_epochs[None, :] % entry_total
    angle = rotation_radians.astype(jnp.float32) * (2.0 * math.pi / entry_total)
    factor = 1.0 / math.sqrt(entry_total)
    cosine = jnp.cos(angle) * factor
    sine = jnp.sin(angle) * factor
    upper = jnp.concatenate([cosine, sine], axis=1)
    lower = jnp.concatenate([-sine, cosine], axis=1)
    return jnp.concatenate([upper, lower], axis=0).astype(jnp.bfloat16)


def couple(own, partners, offsets, frame_count):
    own_count, _, harmonic_degree_total = own.shape
    offset_count = offsets.shape[0]
    epochs = jnp.arange(frame_count, dtype=jnp.int32)
    source = (epochs[None, :, None] - offsets[:, None, None]) % frame_count
    selector = (epochs[None, None, :] == source).astype(jnp.bfloat16)
    halves = own.reshape(own_count, 2, frame_count, harmonic_degree_total)
    shifted = jnp.einsum("kwv,oqvl->okqwl", selector, halves, preferred_element_type=jnp.float32)
    shifted = shifted.astype(jnp.bfloat16).reshape(
        own_count, offset_count, 2 * frame_count, harmonic_degree_total
    )
    imag_part = jnp.concatenate(
        [partners[:, :, frame_count:], -partners[:, :, :frame_count]], axis=2
    )
    both = jnp.concatenate([partners, imag_part], axis=3)
    scale = 1.0 / math.sqrt(frame_count)
    results = []
    for partner_index in range(2):
        product = jnp.einsum(
            "okrl,orm->oklm", shifted, both[:, partner_index], preferred_element_type=jnp.float32
        )
        results.append((product * scale).astype(jnp.bfloat16))
    stacked = jnp.stack(results, axis=1)
    return stacked.reshape(
        own_count, 2, offset_count, harmonic_degree_total, 2, harmonic_degree_total
    )


def shards(frames, projection, degree_range, offsets):
    frame_rows, lat_rows, lon_count = frames.shape
    resident_wavenumbers, colatitude_total, harmonic_degree_total = projection.shape
    tm_count = lax.axis_size("tm")
    latitude_groups = lax.axis_size("lat")
    frame_count = frame_rows * tm_count
    azimuthal_order_count = resident_wavenumbers * tm_count * latitude_groups
    slots = jnp.arange(azimuthal_order_count, dtype=jnp.int32)
    table = longitude_table(lon_count, slots)
    azimuthal = jnp.dot(
        frames.reshape(frame_rows * lat_rows, lon_count), table, preferred_element_type=jnp.float32
    )
    azimuthal = azimuthal.astype(jnp.bfloat16).reshape(
        frame_rows, lat_rows, 2 * azimuthal_order_count
    )
    moved = lax.all_to_all(azimuthal[None], ("tm", "lat"), split_axis=3, concat_axis=0, tiled=True)
    grid = moved.reshape(tm_count, latitude_groups, frame_rows, lat_rows, resident_wavenumbers, 2)
    bands = projection.reshape(
        resident_wavenumbers, latitude_groups, lat_rows, harmonic_degree_total
    )
    summed = jnp.einsum("ijtaop,ojal->opitl", grid, bands, preferred_element_type=jnp.float32)
    summed = summed.reshape(resident_wavenumbers, 2, frame_count, harmonic_degree_total)
    device_rank = lax.axis_index("tm") * latitude_groups + lax.axis_index("lat")
    bounds = lax.dynamic_slice_in_dim(
        degree_range, device_rank * resident_wavenumbers, resident_wavenumbers, 0
    )
    degrees = jnp.arange(harmonic_degree_total, dtype=jnp.int32)
    keep = ((degrees[None, :] >= bounds[:, 0:1]) & (degrees[None, :] < bounds[:, 1:2])).astype(
        jnp.float32
    )
    harmonic = (summed * keep[:, None, None, :]).astype(jnp.bfloat16)
    harmonic = harmonic.reshape(resident_wavenumbers, 2 * frame_count, harmonic_degree_total)
    transform = time_table(frame_count)
    spectrum = jnp.einsum(
        "wr,orl->owl", transform, harmonic, preferred_element_type=jnp.float32
    ).astype(jnp.bfloat16)
    following = shifted_2(spectrum, ("tm", "lat"), -1)
    combined = jnp.concatenate([spectrum, following], axis=0)
    partners = jnp.stack(
        [combined[1 : resident_wavenumbers + 1], combined[2 : resident_wavenumbers + 2]], axis=1
    )
    return couple(spectrum, partners, offsets, frame_count)


def solution(mesh):
    return jax.shard_map(
        shards,
        mesh=mesh,
        in_specs=(P("tm", "lat", None), P(("tm", "lat"), None, None), P(), P()),
        out_specs=P(("tm", "lat"), None, None, None, None, None),
        check_vma=False,
    )
```

profile of v0, /device:TPU:7, one launch (start us, length us, event | category | flops | bytes accessed | tf_op | source)
XLA Modules:
  0.0 365.4 jit_solution(11914598363188593476)
XLA Ops:
  0.0 0.0 copy-start
  0.0 4.4 %multiply_convert_fusion.2 = (bf16[1024,256,1]{1,0,2:T(8,128)(2,1)S(1)}, bf16[1024,256,1]{1,0,2:T(8,128)(2,1)S(1)}) fusion(), kind=kLoop, calls=%fused_computation.36 | loop fusion | flops 4980736 | bytes 1048576 | tf_op jit(solution)/shard_map/convert.7
  4.4 0.1 pad_maximum_fusion.3
  4.5 2.1 copy.52
  6.6 1.5 convert_element_type.73
  8.1 9.5 %fusion.2 = bf16[4096,512]{0,1:T(8,128)(2,1)} fusion(bf16[1024,512]{0,1:T(8,128)(2,1)S(1)} %convert_element_type.73, bf16[4096,1024]{1,0:T(8,128)(2,1)} %bitcast.90), kind=kOutput, calls=%fused_computation.8 | convolution fusion | flops 4297064448 | bytes 13631488 | tf_op jit(solution)/shard_map/dot_general | solution.py:73
  17.6 6.5 %copy.53 = bf16[4096,512]{1,0:T(8,128)(2,1)} copy(bf16[4096,512]{0,1:T(8,128)(2,1)} %fusion.2) | data formatting | bytes 8388608 | tf_op jit(solution)/shard_map/convert_element_type | solution.py:76
  24.0 12.9 %copy.54 = bf16[1,64,64,512]{2,1,0,3:T(8,128)(2,1)} copy(bf16[1,64,64,512]{3,2,1,0:T(8,128)(2,1)} %bitcast.85) | data formatting | bytes 8388608 | tf_op jit(solution)/shard_map/broadcast_in_dim;reshape | solution.py:79
  36.9 13.9 %reshape.204 = bf16[32,2,32768]{2,1,0:T(2,128)(2,1)} reshape(bf16[512,1,64,64]{3,2,1,0:T(8,128)(2,1)} %bitcast.83) | data formatting | bytes 8388608
  50.8 0.0 copy-start.3
  50.8 6.4 %all-to-all-start = ((bf16[32,2,32768]{2,1,0:T(2,128)(2,1)}), bf16[32,2,32768]{2,1,0:T(2,128)(2,1)}, u32[]{:S(2)}, u32[]{:S(2)}) async-start(bf16[32,2,32768]{2,1,0:T(2,128)(2,1)} %reshape.204), calls=%async_computation | async-start | bytes 8388608 | tf_op jit(solution)/shard_map/all_to_all | solution.py:79
  57.3 0.0 copy-done.3
  57.3 0.1 constant_dynamic-slice_fusion
  57.3 1.0 fusion.33
  58.3 1.1 negate_convert_fusion
  59.5 0.1 fusion.39
  59.5 90.9 %all-to-all-done = bf16[32,2,32768]{2,1,0:T(2,128)(2,1)} async-done(((bf16[32,2,32768]{2,1,0:T(2,128)(2,1)}), bf16[32,2,32768]{2,1,0:T(2,128)(2,1)}, u32[]{:S(2)}, u32[]{:S(2)}) %all-to-all-start) | async-done | bytes 4194336 | tf_op jit(solution)/shard_map/all_to_all | solution.py:79
  150.4 13.6 %reshape.205 = bf16[512,1,64,64]{3,2,1,0:T(8,128)(2,1)} reshape(bf16[32,2,32768]{2,1,0:T(2,128)(2,1)} %all-to-all-done) | data formatting | bytes 8388608
  164.0 12.0 %copy.55 = bf16[1,64,64,512]{2,3,1,0:T(8,128)(2,1)} copy(bf16[1,64,64,512]{2,1,0,3:T(8,128)(2,1)} %bitcast.84) | data formatting | bytes 8388608 | tf_op jit(solution)/shard_map/all_to_all | solution.py:79
  176.0 0.0 copy-done
  176.0 13.5 %fusion.4 = f32[8,2,4,64,256]{4,3,1,2,0:T(8,128)S(1)} fusion(bf16[8,8,64,256,1,1]{3,2,1,5,4,0:T(8,128)(2,1)S(1)} %bitcast.80, bf16[4,8,64,64,8,2]{3,5,4,1,0,2:T(2,128)(2,1)} %bitcast.89), kind=kOutput, calls=%fused_computation.17 | convolution fusion | flops 1073741824 | bytes 10485760 | tf_op jit(solution)/shard_map/ijtaop,ojal->opitl/dot_general | solution.py:84
  189.5 0.3 copy.58
  189.7 0.6 fusion.3
  190.4 0.0 copy-start.2
  190.4 2.6 convert_bitcast_fusion.1
  193.0 2.9 collective-permute-start
  195.9 0.0 copy-done.2
  195.9 0.1 add_select_fusion.2
  196.0 2.8 copy.79
  198.8 4.8 %convert_bitcast_fusion = bf16[8,8,2,256,256]{4,3,1,2,0:T(8,128)(2,1)S(1)} fusion(bf16[8,2,256,256,1]{3,2,4,1,0:T(8,128)(2,1)S(1)} %bitcast.88, s32[8,256]{1,0:T(8,128)S(1)} %add_select_fusion.2), kind=kOutput, calls=%fused_computation.3 | convolution fusion | flops 4303880192 | bytes 18882560 | tf_op jit(solution)/shard_map/kwv,oqvl->okqwl/dot_general | solution.py:43
  203.7 6.6 %copy.61 = bf16[8,8,2,256,256]{4,3,2,1,0:T(8,128)(2,1)} copy(bf16[8,8,2,256,256]{4,3,1,2,0:T(8,128)(2,1)S(1)} %convert_bitcast_fusion) | data formatting | bytes 33554432 | tf_op jit(solution)/shard_map/convert_element_type | solution.py:44
  210.2 12.3 %collective-permute-done = bf16[8,512,256]{1,2,0:T(8,128)(2,1)} collective-permute-done((bf16[8,512,256]{1,2,0:T(8,128)(2,1)}, bf16[8,512,256]{1,2,0:T(8,128)(2,1)}, u32[]{:S(2)}, u32[]{:S(2)}) %collective-permute-start) | collective-permute-done | bytes 2097184 | tf_op jit(solution)/shard_map/ppermute | solution.py:12
  222.5 2.3 fusion.9
  224.8 0.6 fusion.7
  225.4 3.6 maximum_maximum_fusion
  229.1 17.3 %multiply_convert_fusion = bf16[8,8,256,512]{3,2,1,0:T(8,128)(2,1)} fusion(bf16[8,8,512,256]{3,2,1,0:T(8,128)(2,1)} %bitcast.86, bf16[8,2,512,512]{2,3,0,1:T(8,128)(2,1)} %maximum_maximum_fusion), kind=kOutput, calls=%fused_computation.1 | convolution fusion | flops 8606711808 | bytes 37748736 | tf_op jit(solution)/shard_map/okrl,orm->oklm/dot_general | solution.py:54
  246.4 17.3 %multiply_convert_fusion.1 = bf16[8,8,256,512]{3,2,1,0:T(8,128)(2,1)} fusion(bf16[8,8,512,256]{3,2,1,0:T(8,128)(2,1)} %bitcast.87, bf16[8,2,512,512]{2,3,0,1:T(8,128)(2,1)} %maximum_maximum_fusion), kind=kOutput, calls=%fused_computation.2 | convolution fusion | flops 8606711808 | bytes 37748736 | tf_op jit(solution)/shard_map/okrl,orm->oklm/dot_general | solution.py:54
  263.7 23.8 %stack.28 = bf16[8,1,8,256,2,256]{5,4,3,2,0,1:T(2,128)(2,1)} reshape(bf16[8,8,256,512]{3,2,1,0:T(8,128)(2,1)} %multiply_convert_fusion.1) | data formatting | bytes 33554432 | tf_op jit(solution)/shard_map/stack | solution.py:58
  287.5 23.8 %stack.29 = bf16[8,1,8,256,2,256]{5,4,3,2,0,1:T(2,128)(2,1)} reshape(bf16[8,8,256,512]{3,2,1,0:T(8,128)(2,1)} %multiply_convert_fusion) | data formatting | bytes 33554432 | tf_op jit(solution)/shard_map/stack | solution.py:58
  311.2 0.0 copy-start.1
  311.2 54.0 %pad_maximum_fusion = bf16[8,2,8,256,2,256]{5,4,3,2,1,0:T(2,128)(2,1)} fusion(bf16[8,1,8,256,2,256]{5,4,3,2,1,0:T(2,128)(2,1)} %bitcast.82, bf16[8,1,8,256,2,256]{5,4,3,2,1,0:T(2,128)(2,1)} %bitcast.81), kind=kLoop, calls=%fused_computation | loop fusion | flops 16777216 | bytes 67108864 | tf_op jit(solution)/shard_map/stack | solution.py:58
  365.3 0.0 copy-done.1
  (1 shorter events, 0.0 us)
Async XLA Ops:
  0.0 176.0 %copy-start = (bf16[8,512,256]{2,1,0:T(8,128)(2,1)S(1)}, bf16[8,512,256]{2,1,0:T(8,128)(2,1)}, u32[]{:S(2)}) copy-start(bf16[8,512,256]{2,1,0:T(8,128)(2,1)} %param.5) | copy-start | bytes 6291460
  50.8 6.4 %copy-start.3 = (s32[256,2]{0,1:T(2,128)S(1)}, s32[256,2]{0,1:T(2,128)}, u32[]{:S(2)}) copy-start(s32[256,2]{0,1:T(2,128)} %param.6) | copy-start | bytes 6148
  50.8 99.6 %all-to-all-start = ((bf16[32,2,32768]{2,1,0:T(2,128)(2,1)}), bf16[32,2,32768]{2,1,0:T(2,128)(2,1)}, u32[]{:S(2)}, u32[]{:S(2)}) async-start(bf16[32,2,32768]{2,1,0:T(2,128)(2,1)} %reshape.204), calls=%async_computation | async-start | bytes 8388608 | tf_op jit(solution)/shard_map/all_to_all | solution.py:79
  190.4 5.5 %copy-start.2 = (s32[8]{0:T(128)S(1)}, s32[8]{0:T(128)}, u32[]{:S(2)}) copy-start(s32[8]{0:T(128)} %param.7) | copy-start | bytes 100
  193.0 29.5 %collective-permute-start = (bf16[8,512,256]{1,2,0:T(8,128)(2,1)}, bf16[8,512,256]{1,2,0:T(8,128)(2,1)}, u32[]{:S(2)}, u32[]{:S(2)}) collective-permute-start(bf16[8,512,256]{1,2,0:T(8,128)(2,1)} %convert_bitcast_fusion.1), channel_id=1, source_target_pairs={{1,0},{2,1},{3,2},{4,3},{5,4},{6,5},{7,6},{8,7},{9,8},{10,9},{11,1... | collective-permute-start | bytes 6291464 | tf_op jit(solution)/shard_map/ppermute | solution.py:12
  311.2 54.0 %copy-start.1 = (bf16[8,512,256]{2,1,0:T(8,128)(2,1)S(1)}, bf16[8,512,256]{2,1,0:T(8,128)(2,1)}, u32[]{:S(2)}) copy-start(bf16[8,512,256]{2,1,0:T(8,128)(2,1)} %param.5) | copy-start | bytes 6291460
where the time goes:
time: 368 us; the launch traced here: 365 us
  local copies, waits for them, and re-layouts  120 us (33%)
  waiting for transfers between devices  103 us (28%)
  other arithmetic  68 us (18%)
  matrix products  65 us (18%)
  starting transfers between devices  9.27 us (3%)
    all_to_all x1, waiting for transfers between devices, shards(): lax.all_to_all(azimuthal[None], ('tm', 'lat'), split_axis=3, concat_axis=...  90.9 us
    another operation x1, other arithmetic, couple(): stacked = jnp.stack(results, axis=1)  54 us
    another operation x2, local copies, waits for them, and re-layouts, couple(): stacked = jnp.stack(results, axis=1)  47.5 us
    dot_general x2, matrix products, couple(): jnp.einsum('okrl,orm->oklm', shifted, both[:, partner_index], preferred_e...  34.6 us
    unnamed x10, local copies, waits for them, and re-layouts  27.5 us
    dot_general x1, matrix products, shards(): jnp.einsum('ijtaop,ojal->opitl', grid, bands, preferred_element_type=jnp....  13.5 us
    another operation x1, local copies, waits for them, and re-layouts, shards(): azimuthal[None]  12.9 us
    ppermute x1, waiting for transfers between devices, shifted_2(): return lax.ppermute(block, axis, route)  12.3 us
  transfers between devices with their start and end apart: 2, of which 2 were waited for; matrix products, arithmetic and copies ran while one was open for 5% of the time, Pallas kernels for 0%

commit v1 on v0

v1 whole, which is shorter than its diff:
```python
import functools
import math

import jax
import jax.numpy as jnp
import numpy as np
from jax import lax
from jax.experimental import pallas as pl
from jax.experimental.pallas import tpu as pltpu
from jax.sharding import PartitionSpec as P

LANES = 128
CHUNK = 2
VMEM_LIMIT = 60 * 1024 * 1024


def shifted(block, axis, distance):
    devices = range(lax.axis_size(axis))
    route = [(i - distance, i) for i in devices if i - distance in devices]
    return lax.ppermute(block, axis, route)


def longitude_rows(lon_count, order_ids):
    phase = np.asarray(order_ids, np.int64)[:, None] * np.arange(lon_count)[None, :] % lon_count
    angle = phase * (2.0 * math.pi / lon_count)
    factor = 1.0 / math.sqrt(lon_count)
    table = np.stack([np.cos(angle) * factor, -np.sin(angle) * factor], axis=1)
    return jnp.asarray(table.reshape(-1, lon_count).astype(np.float32)).astype(jnp.bfloat16)


def azimuthal_kernel(chunks, table_ref, frames_ref, *out_refs):
    groups, steps, lat_rows, lon_count = frames_ref.shape
    first = pl.program_id(0) * steps
    width = groups * lat_rows
    for pair in range(0, steps, 2):
        spans = range(pair, min(pair + 2, steps))
        block = jnp.concatenate(
            [frames_ref[:, g].reshape(width, lon_count) for g in spans], axis=0
        )
        for chunk, out_ref in enumerate(out_refs):
            value = lax.dot_general(
                table_ref[chunk],
                block,
                (((1,), (1,)), ((), ())),
                preferred_element_type=jnp.float32,
            ).astype(jnp.bfloat16)
            for n, g in enumerate(spans):
                part = value[:, n * width : (n + 1) * width]
                out_ref[:, first + g] = part.reshape(part.shape[0] // 2, 2, width)


def azimuthal_transform(table, frames, steps):
    chunks, rows, lon_count = table.shape
    groups, times, lat_rows, _ = frames.shape
    shape = (rows // 2, times, 2, groups * lat_rows)
    return pl.pallas_call(
        functools.partial(azimuthal_kernel, chunks),
        grid=(times // steps,),
        in_specs=[
            pl.BlockSpec((chunks, rows, lon_count), lambda i: (0, 0, 0)),
            pl.BlockSpec((groups, steps, lat_rows, lon_count), lambda i: (0, i, 0, 0)),
        ],
        out_specs=[pl.BlockSpec(shape, lambda i: (0, 0, 0, 0)) for _ in range(chunks)],
        out_shape=[jax.ShapeDtypeStruct(shape, jnp.bfloat16) for _ in range(chunks)],
        compiler_params=pltpu.CompilerParams(vmem_limit_bytes=VMEM_LIMIT),
        cost_estimate=pl.CostEstimate(
            flops=2 * chunks * rows * frames.size,
            bytes_accessed=2 * frames.size,
            transcendentals=0,
        ),
    )(table, frames)


def legendre_kernel(groups, bounds_ref, wire_ref, projection_ref, out_ref, wide):
    _, lat_groups, _, rows, lanes = wire_ref.shape
    degrees = projection_ref.shape[-1]
    lat_rows = lanes // groups
    order = pl.program_id(0)

    @pl.when(order == 0)
    def _():
        wide[...] = jnp.zeros_like(wide)

    for a in range(lat_groups):
        band = projection_ref[0, a * lat_rows : (a + 1) * lat_rows, :]
        for g in range(groups):
            start = a * lanes + g * lat_rows
            wide[start : start + lat_rows, g * degrees : (g + 1) * degrees] = band
    tall = wire_ref.shape[0] * rows
    left = jnp.concatenate(
        [wire_ref[:, a, 0].reshape(tall, lanes) for a in range(lat_groups)], axis=1
    )
    lane = lax.broadcasted_iota(jnp.int32, (tall, degrees), 1)
    keep = (lane >= bounds_ref[order, 0]) & (lane < bounds_ref[order, 1])
    for g in range(groups):
        columns = slice(g * degrees, (g + 1) * degrees)
        summed = jnp.dot(left, wide[:, columns], preferred_element_type=jnp.float32)
        out_ref[0, g * tall : (g + 1) * tall, :] = jnp.where(keep, summed, 0.0).astype(jnp.bfloat16)


def legendre(groups, bounds, wire, projection):
    tm_count, lat_groups, orders, rows, lanes = wire.shape
    _, lat_total, degrees = projection.shape
    total = groups * tm_count * rows
    return pl.pallas_call(
        functools.partial(legendre_kernel, groups),
        grid=(orders,),
        in_specs=[
            pl.BlockSpec(memory_space=pltpu.SMEM),
            pl.BlockSpec((tm_count, lat_groups, 1, rows, lanes), lambda o: (0, 0, o, 0, 0)),
            pl.BlockSpec((1, lat_total, degrees), lambda o: (o, 0, 0)),
        ],
        out_specs=pl.BlockSpec((1, total, degrees), lambda o: (o, 0, 0)),
        out_shape=jax.ShapeDtypeStruct((orders, total, degrees), jnp.bfloat16),
        scratch_shapes=[pltpu.VMEM((lat_groups * lanes, groups * degrees), jnp.bfloat16)],
        compiler_params=pltpu.CompilerParams(vmem_limit_bytes=VMEM_LIMIT),
        cost_estimate=pl.CostEstimate(
            flops=2 * wire.size * groups * degrees,
            bytes_accessed=2 * (wire.size + projection.size),
            transcendentals=0,
        ),
    )(bounds, wire, projection)


def couple_kernel(turn_ref, twice_ref, own_ref, next_ref, *rest):
    out_ref, held, flipped, turned = rest[-4:]
    order, k = pl.program_id(0), pl.program_id(1)
    orders, total, degrees = own_ref.shape
    tall = 2 * degrees

    @pl.when(k == 0)
    def _():
        value = lax.dot_general(
            twice_ref[...],
            own_ref[order],
            (((1,), (1,)), ((), ())),
            preferred_element_type=jnp.float32,
        )
        held[...] = value
        lane = lax.broadcasted_iota(jnp.int32, (tall, total), 1)
        flipped[...] = jnp.where(
            lane % 2 == 0, pltpu.roll(value, total - 1, 1), pltpu.roll(value, 1, 1)
        )

    straight, crossed = turn_ref[k, 0][None], turn_ref[k, 1][None]
    x = held[...].reshape(tall // 8, 8, total)
    y = flipped[...].reshape(tall // 8, 8, total)
    turned[...] = (x * straight + y * crossed).reshape(tall, total).astype(jnp.bfloat16)

    def emit(s, partner):
        product = jnp.dot(turned[...], partner, preferred_element_type=jnp.float32)
        out_ref[0, s, 0] = product.astype(jnp.bfloat16).reshape(degrees, 2, degrees)

    for first in range(orders):

        @pl.when(order == first)
        def _():
            for s in range(2):
                other = first + 1 + s
                emit(s, own_ref[other] if other < orders else next_ref[other - orders])


def couple(turn, twice, own, following, out, first, out_shape):
    offsets = turn.shape[0]
    orders, total, degrees = own.shape
    tall = 2 * degrees
    operands = [turn, twice, own, following]
    specs = [
        pl.BlockSpec(turn.shape, lambda o, k: (0, 0, 0, 0)),
        pl.BlockSpec(twice.shape, lambda o, k: (0, 0)),
        pl.BlockSpec(own.shape, lambda o, k: (0, 0, 0)),
        pl.BlockSpec(following.shape, lambda o, k: (0, 0, 0)),
    ]
    aliases = {}
    if out is not None:
        aliases = {len(operands): 0}
        operands.append(out)
        specs.append(pl.BlockSpec(memory_space=pl.ANY))
    return pl.pallas_call(
        couple_kernel,
        grid=(orders, offsets),
        in_specs=specs,
        out_specs=pl.BlockSpec(
            (1, 2, 1, degrees, 2, degrees), lambda o, k: (o + first, 0, k, 0, 0, 0)
        ),
        out_shape=out_shape,
        scratch_shapes=[
            pltpu.VMEM((tall, total), jnp.float32),
            pltpu.VMEM((tall, total), jnp.float32),
            pltpu.VMEM((tall, total), jnp.bfloat16),
        ],
        input_output_aliases=aliases,
        compiler_params=pltpu.CompilerParams(vmem_limit_bytes=VMEM_LIMIT),
        cost_estimate=pl.CostEstimate(
            flops=4 * orders * offsets * total * tall * degrees,
            bytes_accessed=4 * orders * offsets * tall * degrees,
            transcendentals=0,
        ),
    )(*operands)


def phase_turns(offsets, times, frame_count):
    phase = offsets[:, None] * times[None, :] % frame_count
    angle = phase.astype(jnp.float32) * (2.0 * math.pi / frame_count)
    factor = 1.0 / math.sqrt(frame_count)
    cosine, sine = jnp.cos(angle) * factor, jnp.sin(angle) * factor
    straight = jnp.stack(
        [jnp.stack([cosine, cosine], -1), jnp.stack([-sine, -sine], -1)], axis=1
    )
    crossed = jnp.stack(
        [jnp.stack([-sine, sine], -1), jnp.stack([-cosine, cosine], -1)], axis=1
    )
    turns = jnp.stack([straight, crossed], axis=1)
    turns = turns.reshape(offsets.shape[0], 2, 2, -1)
    return jnp.tile(turns, (1, 1, 4, 1))


def shards(frames, projection, degree_range, offsets):
    frame_rows, lat_rows, lon_count = frames.shape
    orders, lat_total, degrees = projection.shape
    tm_count, lat_groups = lax.axis_size("tm"), lax.axis_size("lat")
    devices = tm_count * lat_groups
    frame_count = frame_rows * tm_count
    groups = LANES // lat_rows
    times = frame_rows // groups
    steps = min(4, times)
    chunks = orders // CHUNK

    ids = np.arange(devices * orders).reshape(devices, chunks, CHUNK)
    table = jnp.stack(
        [longitude_rows(lon_count, ids[:, c].reshape(-1)) for c in range(chunks)], axis=0
    )
    grouped = frames.reshape(groups, times, lat_rows, lon_count)
    sent = list(azimuthal_transform(table[:1], grouped, steps))
    if chunks > 1:
        sent += list(azimuthal_transform(table[1:], grouped, steps))

    rank = lax.axis_index("tm") * lat_groups + lax.axis_index("lat")
    bounds = lax.dynamic_slice_in_dim(degree_range, rank * orders, orders, 0)
    time_ids = (
        np.arange(tm_count)[None, :, None] * frame_rows
        + np.arange(groups)[:, None, None] * times
        + np.arange(times)[None, None, :]
    ).reshape(-1)
    turn = phase_turns(offsets, jnp.asarray(time_ids, jnp.int32), frame_count)
    row = lax.broadcasted_iota(jnp.int32, (2 * degrees, degrees), 0)
    column = lax.broadcasted_iota(jnp.int32, (2 * degrees, degrees), 1)
    twice = (row // 2 == column).astype(jnp.bfloat16)

    harmonics = []
    for c in range(chunks):
        packed = sent[c].reshape(devices, CHUNK * times * 2, LANES)
        moved = lax.all_to_all(packed, ("tm", "lat"), split_axis=0, concat_axis=0, tiled=True)
        wire = moved.reshape(tm_count, lat_groups, CHUNK, times * 2, LANES)
        own = slice(c * CHUNK, (c + 1) * CHUNK)
        harmonics.append(legendre(groups, bounds[own], wire, projection[own]))
    harmonics.append(shifted(harmonics[0], ("tm", "lat"), -1))
    shape = jax.ShapeDtypeStruct(
        (orders, 2, offsets.shape[0], degrees, 2, degrees), jnp.bfloat16
    )
    out = None
    for c in range(chunks):
        out = couple(turn, twice, harmonics[c], harmonics[c + 1], out, c * CHUNK, shape)
    return out


def solution(mesh):
    return jax.shard_map(
        shards,
        mesh=mesh,
        in_specs=(P("tm", "lat", None), P(("tm", "lat"), None, None), P(), P()),
        out_specs=P(("tm", "lat"), None, None, None, None, None),
        check_vma=False,
    )
```

time: 368 us -> 190 us (0.52)
  local copies, waits for them, and re-layouts: 120 us -> 9.44 us
  Pallas kernels: 0 us -> 91.8 us
  waiting for transfers between devices: 103 us -> 36.5 us
  other arithmetic: 68 us -> 1.82 us
  matrix products: 65 us -> 0 us
  blocking collectives: 0 us -> 29.9 us
  starting transfers between devices: 9.27 us -> 17.8 us
    pallas_call x0 -> x10, Pallas kernels: none -> 91.8 us  [the longest x4 58.8 us: couple(): pl.pallas_call(couple_kernel, grid=(orders, offsets), in_specs=specs, out...]
    dot_general x6 -> x0, matrix products: 65 us -> none  [the longest x2 34.6 us: couple(): jnp.einsum('okrl,orm->oklm', shifted, both[:, partner_index], preferred_e...]
    another operation x7 -> x2, other arithmetic: 63.6 us -> 0.01 us  [the longest x1 0.01 us: phase_turns(): return jnp.tile(turns, (1, 1, 4, 1))]
    another operation x4 -> x11, local copies, waits for them, and re-layouts: 62.5 us -> 2.06 us  [the longest x3 1.03 us: phase_turns(): return jnp.tile(turns, (1, 1, 4, 1))]
    all_to_all x1 -> x3, waiting for transfers between devices: 90.9 us -> 36.5 us  [shards(): lax.all_to_all(packed, ('tm', 'lat'), split_axis=0, concat_axis=0, tiled=...]
    all_to_all x0 -> x1, blocking collectives: none -> 29.9 us  [shards(): lax.all_to_all(packed, ('tm', 'lat'), split_axis=0, concat_axis=0, tiled=...]
    unnamed x10 -> x14, local copies, waits for them, and re-layouts: 27.5 us -> 4.34 us
    convert_element_type x3 -> x0, local copies, waits for them, and re-layouts: 14.5 us -> none  [the longest x1 6.56 us: couple(): shifted.astype(jnp.bfloat16)]
  transfers between devices with their start and end apart: 2 -> 4, of which waited for: 2 -> 2; matrix products, arithmetic and copies ran while one was open for 5% -> 5% of each run, Pallas kernels for 0% -> 36%
where the time goes in v1:
time: 190 us; the launch traced here: 187 us
  Pallas kernels  91.8 us (48%)
  waiting for transfers between devices  36.5 us (19%)
  blocking collectives  29.9 us (16%)
  starting transfers between devices  17.8 us (9%)
  local copies, waits for them, and re-layouts  9.44 us (5%)
    pallas_call x4, Pallas kernels, couple(): pl.pallas_call(couple_kernel, grid=(orders, offsets), in_specs=specs, out...  58.8 us
    all_to_all x3, waiting for transfers between devices, shards(): lax.all_to_all(packed, ('tm', 'lat'), split_axis=0, concat_axis=0, tiled=...  36.5 us
    all_to_all x1, blocking collectives, shards(): lax.all_to_all(packed, ('tm', 'lat'), split_axis=0, concat_axis=0, tiled=...  29.9 us
    pallas_call x2, Pallas kernels, azimuthal_transform(): pl.pallas_call(functools.partial(azimuthal_kernel, chunks), grid=(times /...  22 us
    all_to_all x3, starting transfers between devices, shards(): lax.all_to_all(packed, ('tm', 'lat'), split_axis=0, concat_axis=0, tiled=...  15.5 us
    pallas_call x4, Pallas kernels, legendre(): pl.pallas_call(functools.partial(legendre_kernel, groups), grid=(orders,)...  11.1 us
    unnamed x14, local copies, waits for them, and re-layouts  4.34 us
  transfers between devices with their start and end apart: 4, of which 2 were waited for; matrix products, arithmetic and copies ran while one was open for 5% of the time, Pallas kernels for 36%

profile of v1, /device:TPU:7, one launch (start us, length us, event | category | flops | bytes accessed | tf_op | source)
XLA Modules:
  0.0 187.5 jit_solution(4769129996294184875)
XLA Ops:
  0.0 0.0 copy-start
  0.0 8.9 %shard_map.93 = bf16[64,32,2,128]{3,2,1,0:T(2,128)(2,1)} custom-call(bf16[1,128,1024]{2,1,0:T(8,128)(2,1)} %constant.71.table_ref, bf16[2,32,64,1024]{3,2,1,0:T(8,128)(2,1)} %bitcast.15), custom_call_target="tpu_custom_call" | custom-call | flops 1073741824 | bytes 8388608 | tf_op jit(solution)/shard_map/pallas_call | solution.py:56
  8.9 6.4 %all-to-all-start.1 = ((bf16[32,128,128]{2,1,0:T(8,128)(2,1)}), bf16[32,128,128]{2,1,0:T(8,128)(2,1)S(1)}, u32[]{:S(2)}, u32[]{:S(2)}) async-start(bf16[32,128,128]{2,1,0:T(8,128)(2,1)} %bitcast.17), calls=%async_computation.1 | async-start | bytes 2097152 | tf_op jit(solution)/shard_map/all_to_all | solution.py:253
  15.3 13.1 %shard_map.91 = (bf16[64,32,2,128]{3,2,1,0:T(2,128)(2,1)}, bf16[64,32,2,128]{3,2,1,0:T(2,128)(2,1)}, bf16[64,32,2,128]{3,2,1,0:T(2,128)(2,1)}) custom-call(bf16[3,128,1024]{2,1,0:T(8,128)(2,1)} %constant.69.table_ref, bf16[2,32,64,1024]{3,2,1,0:T(8,128)(2,1)} %bitcast.16), custom_call_target="tpu_custom_call" | custom-call | flops 3221225472 | bytes 8388608 | tf_op jit(solution)/shard_map/pallas_call | solution.py:56
  28.3 12.2 %all-to-all-done.1 = bf16[32,128,128]{2,1,0:T(8,128)(2,1)S(1)} async-done(((bf16[32,128,128]{2,1,0:T(8,128)(2,1)}), bf16[32,128,128]{2,1,0:T(8,128)(2,1)S(1)}, u32[]{:S(2)}, u32[]{:S(2)}) %all-to-all-start.1) | async-done | bytes 1048608 | tf_op jit(solution)/shard_map/all_to_all | solution.py:253
  40.5 0.0 copy-start.1
  40.5 29.9 %all_to_all.20 = bf16[32,128,128]{2,1,0:T(8,128)(2,1)} all-to-all(bf16[32,128,128]{2,1,0:T(8,128)(2,1)} %bitcast.24), channel_id=1, replica_groups=mesh['tm'=4,'lat'=8] {'tm','lat'}, dimensions={0} | all-to-all | bytes 2097152 | tf_op jit(solution)/shard_map/all_to_all | solution.py:253
  70.4 4.6 %all-to-all-start.3 = ((bf16[32,128,128]{2,1,0:T(8,128)(2,1)}), bf16[32,128,128]{2,1,0:T(8,128)(2,1)S(1)}, u32[]{:S(2)}, u32[]{:S(2)}) async-start(bf16[32,128,128]{2,1,0:T(8,128)(2,1)} %bitcast.23), calls=%async_computation.3 | async-start | bytes 2097152 | tf_op jit(solution)/shard_map/all_to_all | solution.py:253
  75.0 0.0 copy-done
  75.0 0.1 constant_dynamic-slice_fusion
  75.1 0.8 sine_multiply_fusion
  75.9 24.4 %all-to-all-done.3 = bf16[32,128,128]{2,1,0:T(8,128)(2,1)S(1)} async-done(((bf16[32,128,128]{2,1,0:T(8,128)(2,1)}), bf16[32,128,128]{2,1,0:T(8,128)(2,1)S(1)}, u32[]{:S(2)}, u32[]{:S(2)}) %all-to-all-start.3) | async-done | bytes 1048608 | tf_op jit(solution)/shard_map/all_to_all | solution.py:253
  100.3 0.0 copy-start.2
  100.3 4.6 %all-to-all-start = ((bf16[32,128,128]{2,1,0:T(8,128)(2,1)}), bf16[32,128,128]{2,1,0:T(8,128)(2,1)S(1)}, u32[]{:S(2)}, u32[]{:S(2)}) async-start(bf16[32,128,128]{2,1,0:T(8,128)(2,1)} %bitcast.22), calls=%async_computation | async-start | bytes 2097152 | tf_op jit(solution)/shard_map/all_to_all | solution.py:253
  104.9 0.1 fusion.10
  104.9 0.6 copy.30.bounds_ref
  105.6 0.6 copy.29.bounds_ref
  106.2 0.6 copy.28.bounds_ref
  106.8 0.7 copy.27.bounds_ref
  107.5 0.2 copy.16
  107.7 0.1 copy.18
  107.7 0.2 copy.21
  107.9 0.1 copy.23
  108.0 0.2 copy.20
  108.2 0.1 copy.22
  108.3 0.2 copy.17
  108.5 0.1 copy.19
  108.6 0.1 copy.24
  108.6 0.1 tile.11
  108.7 0.9 tile.12.turn_ref
  109.6 1.0 fusion.twice_ref
  110.6 2.9 %fusion.9 = (bf16[2,512,256]{2,1,0:T(8,128)(2,1)}, bf16[2,512,256]{2,1,0:T(8,128)(2,1)}, bf16[2,512,256]{2,1,0:T(8,128)(2,1)}, bf16[2,512,256]{2,1,0:T(8,128)(2,1)}) fusion(bf16[8,512,256]{2,1,0:T(8,128)(2,1)} %param.10), kind=kLoop, calls=%fused_computation.27 | loop fusion | bytes 4194304 | tf_op jit(solution)/shard_map/slice | solution.py:256
  113.5 0.0 copy-done.1
  113.5 2.8 %shard_map.94.own_ref = bf16[2,512,256]{2,1,0:T(8,128)(2,1)} custom-call(s32[2,2]{1,0:T(2,128)} %copy.28.bounds_ref, bf16[4,8,2,64,128]{4,3,2,1,0:T(8,128)(2,1)} %bitcast.18, bf16[2,512,256]{2,1,0:T(8,128)(2,1)} %get-tuple-element.12.projection_ref), custom_call_target="tpu_custom_call" | custom-call | flops 536870912 | bytes 1572864 | tf_op jit(solution)/shard_map/pallas_call | solution.py:105
  116.3 2.3 %collective-permute-start = (bf16[2,512,256]{2,1,0:T(8,128)(2,1)}, bf16[2,512,256]{2,1,0:T(8,128)(2,1)S(1)}, u32[]{:S(2)}, u32[]{:S(2)}) collective-permute-start(bf16[2,512,256]{2,1,0:T(8,128)(2,1)} %shard_map.94.own_ref), channel_id=1, source_target_pairs={{1,0},{2,1},{3,2},{4,3},{5,4},{6,5},{7,6},{8,7},{9,8},{10,9},{11,1... | collective-permute-start | bytes 1572872 | tf_op jit(solution)/shard_map/ppermute | solution.py:20
  118.6 2.8 %shard_map.95.next_ref.own_ref = bf16[2,512,256]{2,1,0:T(8,128)(2,1)} custom-call(s32[2,2]{1,0:T(2,128)} %copy.29.bounds_ref, bf16[4,8,2,64,128]{4,3,2,1,0:T(8,128)(2,1)} %bitcast.20, bf16[2,512,256]{2,1,0:T(8,128)(2,1)} %get-tuple-element.14.projection_ref), custom_call_target="tpu_custom_call" | custom-call | flops 536870912 | bytes 1572864 | tf_op jit(solution)/shard_map/pallas_call | solution.py:105
  121.4 0.0 copy-done.2
  121.4 2.8 %shard_map.96.next_ref.own_ref = bf16[2,512,256]{2,1,0:T(8,128)(2,1)} custom-call(s32[2,2]{1,0:T(2,128)} %copy.30.bounds_ref, bf16[4,8,2,64,128]{4,3,2,1,0:T(8,128)(2,1)} %bitcast.19, bf16[2,512,256]{2,1,0:T(8,128)(2,1)} %get-tuple-element.11.projection_ref), custom_call_target="tpu_custom_call" | custom-call | flops 536870912 | bytes 1572864 | tf_op jit(solution)/shard_map/pallas_call | solution.py:105
  124.2 14.7 %shard_map.97.rest_0_ = bf16[8,2,8,256,2,256]{5,4,3,2,1,0:T(2,128)(2,1)} custom-call(f32[8,2,8,512]{3,2,1,0:T(8,128)} %tile.12.turn_ref, bf16[512,256]{1,0:T(8,128)(2,1)} %fusion.twice_ref, bf16[2,512,256]{2,1,0:T(8,128)(2,1)} %shard_map.94.own_ref, bf16[2,512,256]{2,1,0:T(8,128)(2,1)} %shard_map.96.next_ref.own_ref), custom_call_target="tpu_custom_call" | custom-call | flops 4294967296 | bytes 8388608 | tf_op jit(solution)/shard_map/pallas_call | solution.py:179
  138.8 14.7 %shard_map.98.rest_0_ = bf16[8,2,8,256,2,256]{5,4,3,2,1,0:T(2,128)(2,1)} custom-call(f32[8,2,8,512]{3,2,1,0:T(8,128)} %tile.12.turn_ref, bf16[512,256]{1,0:T(8,128)(2,1)} %fusion.twice_ref, bf16[2,512,256]{2,1,0:T(8,128)(2,1)} %shard_map.96.next_ref.own_ref, bf16[2,512,256]{2,1,0:T(8,128)(2,1)} %shard_map.95.next_ref.own_ref, ...), custom_call_target="tpu_custom_call", output_to_operand_aliasing={{}: (4, {})} | custom-call | flops 4294967296 | bytes 8388608 | tf_op jit(solution)/shard_map/pallas_call | solution.py:179
  153.5 0.0 all-to-all-done
  153.5 0.0 copy-start.3
  153.5 1.0 copy-done.3
  154.5 2.8 %shard_map.92.next_ref.own_ref = bf16[2,512,256]{2,1,0:T(8,128)(2,1)} custom-call(s32[2,2]{1,0:T(2,128)} %copy.27.bounds_ref, bf16[4,8,2,64,128]{4,3,2,1,0:T(8,128)(2,1)} %bitcast.21, bf16[2,512,256]{2,1,0:T(8,128)(2,1)} %get-tuple-element.13.projection_ref), custom_call_target="tpu_custom_call" | custom-call | flops 536870912 | bytes 1572864 | tf_op jit(solution)/shard_map/pallas_call | solution.py:105
  157.3 14.7 %shard_map.99.rest_0_ = bf16[8,2,8,256,2,256]{5,4,3,2,1,0:T(2,128)(2,1)} custom-call(f32[8,2,8,512]{3,2,1,0:T(8,128)} %tile.12.turn_ref, bf16[512,256]{1,0:T(8,128)(2,1)} %fusion.twice_ref, bf16[2,512,256]{2,1,0:T(8,128)(2,1)} %shard_map.95.next_ref.own_ref, bf16[2,512,256]{2,1,0:T(8,128)(2,1)} %shard_map.92.next_ref.own_ref, ...), custom_call_target="tpu_custom_call", output_to_operand_aliasing={{}: (4, {})} | custom-call | flops 4294967296 | bytes 8388608 | tf_op jit(solution)/shard_map/pallas_call | solution.py:179
  172.0 0.0 collective-permute-done.next_ref
  172.0 0.0 copy-start.4
  172.0 0.8 copy-done.4
  172.8 14.7 %shard_map.100 = bf16[8,2,8,256,2,256]{5,4,3,2,1,0:T(2,128)(2,1)} custom-call(f32[8,2,8,512]{3,2,1,0:T(8,128)} %tile.12.turn_ref, bf16[512,256]{1,0:T(8,128)(2,1)} %fusion.twice_ref, bf16[2,512,256]{2,1,0:T(8,128)(2,1)} %shard_map.92.next_ref.own_ref, bf16[2,512,256]{2,1,0:T(8,128)(2,1)} %copy-done.4, ...), custom_call_target="tpu_custom_call", output_to_operand_aliasing={{}: (4, {})} | custom-call | flops 4294967296 | bytes 8388608 | tf_op jit(solution)/shard_map/pallas_call | solution.py:179
  (4 shorter events, 0.0 us)
Async XLA Ops:
  0.0 75.0 %copy-start = (s32[256,2]{0,1:T(2,128)S(1)}, s32[256,2]{0,1:T(2,128)}, u32[]{:S(2)}) copy-start(s32[256,2]{0,1:T(2,128)} %param.11) | copy-start | bytes 6148
  8.9 31.6 %all-to-all-start.1 = ((bf16[32,128,128]{2,1,0:T(8,128)(2,1)}), bf16[32,128,128]{2,1,0:T(8,128)(2,1)S(1)}, u32[]{:S(2)}, u32[]{:S(2)}) async-start(bf16[32,128,128]{2,1,0:T(8,128)(2,1)} %bitcast.17), calls=%async_computation.1 | async-start | bytes 2097152 | tf_op jit(solution)/shard_map/all_to_all | solution.py:253
  40.5 73.0 %copy-start.1 = (bf16[32,128,128]{2,1,0:T(8,128)(2,1)}, bf16[32,128,128]{2,1,0:T(8,128)(2,1)S(1)}, u32[]{:S(2)}) copy-start(bf16[32,128,128]{2,1,0:T(8,128)(2,1)S(1)} %all-to-all-done.1) | copy-start | bytes 3145732
  70.4 29.8 %all-to-all-start.3 = ((bf16[32,128,128]{2,1,0:T(8,128)(2,1)}), bf16[32,128,128]{2,1,0:T(8,128)(2,1)S(1)}, u32[]{:S(2)}, u32[]{:S(2)}) async-start(bf16[32,128,128]{2,1,0:T(8,128)(2,1)} %bitcast.23), calls=%async_computation.3 | async-start | bytes 2097152 | tf_op jit(solution)/shard_map/all_to_all | solution.py:253
  100.3 21.1 %copy-start.2 = (bf16[32,128,128]{2,1,0:T(8,128)(2,1)}, bf16[32,128,128]{2,1,0:T(8,128)(2,1)S(1)}, u32[]{:S(2)}) copy-start(bf16[32,128,128]{2,1,0:T(8,128)(2,1)S(1)} %all-to-all-done.3) | copy-start | bytes 3145732
  100.3 53.2 %all-to-all-start = ((bf16[32,128,128]{2,1,0:T(8,128)(2,1)}), bf16[32,128,128]{2,1,0:T(8,128)(2,1)S(1)}, u32[]{:S(2)}, u32[]{:S(2)}) async-start(bf16[32,128,128]{2,1,0:T(8,128)(2,1)} %bitcast.22), calls=%async_computation | async-start | bytes 2097152 | tf_op jit(solution)/shard_map/all_to_all | solution.py:253
  116.3 55.7 %collective-permute-start = (bf16[2,512,256]{2,1,0:T(8,128)(2,1)}, bf16[2,512,256]{2,1,0:T(8,128)(2,1)S(1)}, u32[]{:S(2)}, u32[]{:S(2)}) collective-permute-start(bf16[2,512,256]{2,1,0:T(8,128)(2,1)} %shard_map.94.own_ref), channel_id=1, source_target_pairs={{1,0},{2,1},{3,2},{4,3},{5,4},{6,5},{7,6},{8,7},{9,8},{10,9},{11,1... | collective-permute-start | bytes 1572872 | tf_op jit(solution)/shard_map/ppermute | solution.py:20
  153.5 1.0 copy-start.3
  172.0 0.8 copy-start.4

commit v2 on v1

v2 whole, which is shorter than its diff:
```python
import functools
import math

import jax
import jax.numpy as jnp
import numpy as np
from jax import lax
from jax.experimental import pallas as pl
from jax.experimental.pallas import tpu as pltpu
from jax.sharding import PartitionSpec as P

LANES = 128
VMEM_LIMIT = 60 * 1024 * 1024


def chunk_sizes(orders):
    if orders < 4:
        return [orders]
    return [orders // 2, orders - orders // 2 - 1, 1]


def shifted(block, axis, distance):
    devices = range(lax.axis_size(axis))
    route = [(i - distance, i) for i in devices if i - distance in devices]
    return lax.ppermute(block, axis, route)


def longitude_rows(lon_count, order_ids):
    phase = np.asarray(order_ids, np.int64)[:, None] * np.arange(lon_count)[None, :] % lon_count
    angle = phase * (2.0 * math.pi / lon_count)
    factor = 1.0 / math.sqrt(lon_count)
    table = np.stack([np.cos(angle) * factor, -np.sin(angle) * factor], axis=1)
    return jnp.asarray(table.reshape(-1, lon_count).astype(np.float32)).astype(jnp.bfloat16)


def azimuthal_kernel(steps, count, *refs):
    table_refs, frames_ref, out_refs = refs[:count], refs[count], refs[count + 1 : 2 * count + 1]
    held, stages = refs[2 * count + 1], refs[2 * count + 2 : 3 * count + 2]
    in_sem, out_sem = refs[-2:]
    groups, times, lat_rows, lon_count = frames_ref.shape
    pieces = times // steps
    width = groups * lat_rows

    def load(i):
        span = pl.ds(i * steps, steps)
        return pltpu.make_async_copy(frames_ref.at[:, span], held.at[:, span], in_sem.at[i])

    def save(c, i):
        span = pl.ds(i * steps, steps)
        return pltpu.make_async_copy(
            stages[c].at[:, span], out_refs[c].at[:, span], out_sem.at[c, i]
        )

    for i in range(pieces):
        load(i).start()

    def piece(i, carry):
        load(i).wait()
        for pair in range(0, steps, 2):
            spans = range(pair, min(pair + 2, steps))
            block = jnp.concatenate(
                [held[:, i * steps + g].reshape(width, lon_count) for g in spans], axis=0
            )
            for c in range(count):
                value = lax.dot_general(
                    table_refs[c][...],
                    block,
                    (((1,), (1,)), ((), ())),
                    preferred_element_type=jnp.float32,
                ).astype(jnp.bfloat16)
                for n, g in enumerate(spans):
                    part = value[:, n * width : (n + 1) * width]
                    stages[c][:, i * steps + g] = part.reshape(part.shape[0] // 2, 2, width)
        for c in range(count):
            save(c, i).start()
        return carry

    lax.fori_loop(0, pieces, piece, 0)
    for c in range(count):
        for i in range(pieces):
            save(c, i).wait()


def azimuthal_transform(tables, frames, steps):
    count = len(tables)
    groups, times, lat_rows, _ = frames.shape
    shapes = [(t.shape[0] // 2, times, 2, groups * lat_rows) for t in tables]
    return pl.pallas_call(
        functools.partial(azimuthal_kernel, steps, count),
        in_specs=[pl.BlockSpec(memory_space=pltpu.VMEM)] * count
        + [pl.BlockSpec(memory_space=pl.ANY)],
        out_specs=[pl.BlockSpec(memory_space=pl.ANY)] * count,
        out_shape=[jax.ShapeDtypeStruct(s, jnp.bfloat16) for s in shapes],
        scratch_shapes=[pltpu.VMEM(frames.shape, jnp.bfloat16)]
        + [pltpu.VMEM(s, jnp.bfloat16) for s in shapes]
        + [
            pltpu.SemaphoreType.DMA((times // steps,)),
            pltpu.SemaphoreType.DMA((count, times // steps)),
        ],
        compiler_params=pltpu.CompilerParams(vmem_limit_bytes=VMEM_LIMIT),
        cost_estimate=pl.CostEstimate(
            flops=2 * sum(t.shape[0] for t in tables) * frames.size,
            bytes_accessed=2 * frames.size,
            transcendentals=0,
        ),
    )(*tables, frames)


def legendre_kernel(groups, first, bounds_ref, wire_ref, projection_ref, sort_ref, out_ref, wide):
    _, lat_groups, _, rows, lanes = wire_ref.shape
    degrees = projection_ref.shape[-1]
    lat_rows = lanes // groups
    order = pl.program_id(0)

    @pl.when(order == 0)
    def _():
        wide[...] = jnp.zeros_like(wide)

    for a in range(lat_groups):
        band = projection_ref[0, a * lat_rows : (a + 1) * lat_rows, :]
        for g in range(groups):
            start = a * lanes + g * lat_rows
            wide[start : start + lat_rows, g * degrees : (g + 1) * degrees] = band
    tall = wire_ref.shape[0] * rows
    half = tall // 2
    left = jnp.concatenate(
        [wire_ref[:, a, 0].reshape(tall, lanes) for a in range(lat_groups)], axis=1
    )
    lane = lax.broadcasted_iota(jnp.int32, (tall, degrees), 1)
    low, high = bounds_ref[order + first, 0], bounds_ref[order + first, 1]
    keep = (lane >= low) & (lane < high)
    for g in range(groups):
        columns = slice(g * degrees, (g + 1) * degrees)
        summed = jnp.dot(left, wide[:, columns], preferred_element_type=jnp.float32)
        kept = jnp.where(keep, summed, 0.0).astype(jnp.bfloat16)
        parted = jnp.dot(sort_ref[...], kept, preferred_element_type=jnp.float32)
        parted = parted.astype(jnp.bfloat16)
        for q in range(2):
            start = (q * groups + g) * half
            out_ref[0, start : start + half, :] = parted[q * half : (q + 1) * half, :]


def legendre(groups, first, bounds, wire, projection, sort):
    tm_count, lat_groups, orders, rows, lanes = wire.shape
    _, lat_total, degrees = projection.shape
    total = groups * tm_count * rows
    return pl.pallas_call(
        functools.partial(legendre_kernel, groups, first),
        grid=(orders,),
        in_specs=[
            pl.BlockSpec(memory_space=pltpu.SMEM),
            pl.BlockSpec((tm_count, lat_groups, 1, rows, lanes), lambda o: (0, 0, o, 0, 0)),
            pl.BlockSpec((1, lat_total, degrees), lambda o: (o + first, 0, 0)),
            pl.BlockSpec(sort.shape, lambda o: (0, 0)),
        ],
        out_specs=pl.BlockSpec((1, total, degrees), lambda o: (o, 0, 0)),
        out_shape=jax.ShapeDtypeStruct((orders, total, degrees), jnp.bfloat16),
        scratch_shapes=[pltpu.VMEM((lat_groups * lanes, groups * degrees), jnp.bfloat16)],
        compiler_params=pltpu.CompilerParams(vmem_limit_bytes=VMEM_LIMIT),
        cost_estimate=pl.CostEstimate(
            flops=2 * wire.size * groups * degrees,
            bytes_accessed=2 * wire.size,
            transcendentals=0,
        ),
    )(bounds, wire, projection, sort)


def couple_kernel(jobs, turn_ref, twice_ref, *rest):
    out_ref, own, partner, held, turned_a, turned_b = rest[-6:]
    arrays = rest[:-6]
    job, step = pl.program_id(0), pl.program_id(1)
    total, degrees = own.shape
    half = total // 2
    tall = 2 * degrees
    per_step = out_ref.shape[2]
    last = turn_ref.shape[0] - 1

    def turn(k, target):
        u, v = turn_ref[k, 0][None], turn_ref[k, 1][None]
        x = held[:, :half].reshape(tall // 8, 8, half)
        y = held[:, half:].reshape(tall // 8, 8, half)
        target[:, :half] = (x * u + y * v).reshape(tall, half).astype(jnp.bfloat16)
        target[:, half:] = (y * u - x * v).reshape(tall, half).astype(jnp.bfloat16)

    @pl.when(step == 0)
    def _():
        for n, (mine, other) in enumerate(jobs):

            @pl.when(job == n)
            def _():
                own[...] = arrays[mine[0]][mine[1]]
                partner[...] = arrays[other[0]][other[1]]

        held[...] = lax.dot_general(
            twice_ref[...], own[...], (((1,), (1,)), ((), ())), preferred_element_type=jnp.float32
        )
        turn(0, turned_a)

    pair = lax.broadcasted_iota(jnp.int32, (tall // 8, 8, LANES), 1) % 4 < 2
    for i in range(per_step):
        now, later = (turned_a, turned_b) if i % 2 == 0 else (turned_b, turned_a)
        turn(jnp.minimum(step * per_step + i + 1, last), later)
        product = jnp.dot(now[...], partner[...], preferred_element_type=jnp.float32)
        for n in range(degrees // (2 * LANES)):
            a, b = (
                product[:, (2 * n + t) * LANES : (2 * n + t + 1) * LANES].reshape(
                    tall // 8, 8, LANES
                )
                for t in range(2)
            )
            upper = jnp.where(pair, a, pltpu.roll(b, 2, 1))
            lower = jnp.where(pair, pltpu.roll(a, 6, 1), b)
            mixed = jnp.stack([upper, lower], axis=1).reshape(2 * tall, LANES)
            out_ref[0, 0, i] = mixed.astype(jnp.bfloat16)


def couple(turn, twice, arrays, jobs, places, out, shape):
    offsets, degrees = turn.shape[0], twice.shape[1]
    total = arrays[0].shape[1]
    tall = 2 * degrees
    used = sorted({side[0] for job in jobs for side in job})
    jobs = [tuple((used.index(a), n) for a, n in job) for job in jobs]
    per_step = 2
    operands = [turn, twice] + [arrays[a] for a in used]
    specs = [
        pl.BlockSpec(x.shape, functools.partial(lambda d, *_: (0,) * d, x.ndim)) for x in operands
    ]
    aliases = {}
    kernel = functools.partial(couple_kernel, jobs)
    if out is not None:
        aliases = {len(operands) + 1: 0}
        operands.append(out)
        specs.append(pl.BlockSpec(memory_space=pl.ANY))

    def body(places_ref, *refs):
        kernel(*refs)

    return pl.pallas_call(
        body,
        grid_spec=pltpu.PrefetchScalarGridSpec(
            num_scalar_prefetch=1,
            grid=(len(jobs), offsets // per_step),
            in_specs=specs,
            out_specs=pl.BlockSpec(
                (1, 1, per_step, 2 * tall, LANES),
                lambda j, k, places_ref: (places_ref[2 * j], places_ref[2 * j + 1], k, 0, 0),
            ),
            scratch_shapes=[
                pltpu.VMEM((total, degrees), jnp.bfloat16),
                pltpu.VMEM((total, degrees), jnp.bfloat16),
                pltpu.VMEM((tall, total), jnp.float32),
                pltpu.VMEM((tall, total), jnp.bfloat16),
                pltpu.VMEM((tall, total), jnp.bfloat16),
            ],
        ),
        out_shape=shape,
        input_output_aliases=aliases,
        compiler_params=pltpu.CompilerParams(vmem_limit_bytes=VMEM_LIMIT),
        cost_estimate=pl.CostEstimate(
            flops=2 * len(jobs) * offsets * total * tall * degrees,
            bytes_accessed=2 * len(jobs) * offsets * tall * degrees,
            transcendentals=0,
        ),
    )(jnp.asarray(np.asarray(places, np.int32).reshape(-1)), *operands)


def phase_turns(offsets, times, frame_count):
    phase = offsets[:, None] * times[None, :] % frame_count
    angle = phase.astype(jnp.float32) * (2.0 * math.pi / frame_count)
    factor = 1.0 / math.sqrt(frame_count)
    cosine, sine = jnp.cos(angle) * factor, jnp.sin(angle) * factor
    cosine, sine = cosine[:, None, None, :], sine[:, None, None, :]
    which = jnp.arange(2, dtype=jnp.int32)[None, :, None, None]
    part = jnp.arange(8, dtype=jnp.int32)[None, None, :, None] % 2
    return jnp.where(
        which == 0, jnp.where(part == 0, cosine, -sine), jnp.where(part == 0, -sine, -cosine)
    )


def shards(frames, projection, degree_range, offsets):
    frame_rows, lat_rows, lon_count = frames.shape
    orders, _, degrees = projection.shape
    tm_count, lat_groups = lax.axis_size("tm"), lax.axis_size("lat")
    devices = tm_count * lat_groups
    frame_count = frame_rows * tm_count
    groups = LANES // lat_rows
    times = frame_rows // groups
    steps = min(4, times)
    sizes = chunk_sizes(orders)
    starts = [sum(sizes[:c]) for c in range(len(sizes))]

    ids = np.arange(devices * orders).reshape(devices, orders)
    tables = [
        longitude_rows(lon_count, ids[:, a : a + n].reshape(-1)) for a, n in zip(starts, sizes)
    ]
    grouped = frames.reshape(groups, times, lat_rows, lon_count)
    sent = list(azimuthal_transform(tables[:1], grouped, steps))
    if len(sizes) > 1:
        sent += list(azimuthal_transform(tables[1:], grouped, steps))

    rank = lax.axis_index("tm") * lat_groups + lax.axis_index("lat")
    bounds = lax.dynamic_slice_in_dim(degree_range, rank * orders, orders, 0)
    time_ids = (
        np.arange(tm_count)[None, :, None] * frame_rows
        + np.arange(groups)[:, None, None] * times
        + np.arange(times)[None, None, :]
    ).reshape(-1)
    turn = phase_turns(offsets, jnp.asarray(time_ids, jnp.int32), frame_count)
    row = np.arange(2 * degrees)
    degree_of = row // 8 * 4 + np.array([0, 2, 1, 3])[row % 8 // 2]
    twice = jnp.asarray(degree_of[:, None] == np.arange(degrees)[None, :], jnp.bfloat16)
    tall = tm_count * times * 2
    source = np.arange(tall) % (tall // 2) * 2 + np.arange(tall) // (tall // 2)
    sort = jnp.asarray(source[:, None] == np.arange(tall)[None, :], jnp.bfloat16)

    shape = jax.ShapeDtypeStruct(
        (orders, 2, offsets.shape[0], 2 * degrees * degrees // LANES, LANES), jnp.bfloat16
    )
    spot = [(c, n) for c, size in enumerate(sizes) for n in range(size)]
    spot += [(len(sizes), n) for n in range(2)]
    harmonics = [None] * (len(sizes) + 1)
    done = set()
    out = None
    for c, (start, size) in enumerate(zip(starts, sizes)):
        packed = sent[c].reshape(devices, size * times * 2, LANES)
        moved = lax.all_to_all(packed, ("tm", "lat"), split_axis=0, concat_axis=0, tiled=True)
        wire = moved.reshape(tm_count, lat_groups, size, times * 2, LANES)
        harmonics[c] = legendre(groups, start, bounds, wire, projection, sort)
        if c == 0:
            harmonics[-1] = shifted(harmonics[0][:2], ("tm", "lat"), -1)
        end = start + size
        ready = [
            (o, s)
            for o in range(end)
            for s in range(2)
            if (o, s) not in done
            and (o + 1 + s < end or (o + 1 + s >= orders and (c > 0 or c == len(sizes) - 1)))
        ]
        done.update(ready)
        if ready:
            jobs = [(spot[o], spot[o + 1 + s]) for o, s in ready]
            out = couple(turn, twice, harmonics, jobs, ready, out, shape)
    out = out.reshape(
        orders, 2, offsets.shape[0], degrees, degrees // LANES, 2, LANES
    )
    return jnp.swapaxes(out, 4, 5).reshape(orders, 2, offsets.shape[0], degrees, 2, degrees)


def solution(mesh):
    return jax.shard_map(
        shards,
        mesh=mesh,
        in_specs=(P("tm", "lat", None), P(("tm", "lat"), None, None), P(), P()),
        out_specs=P(("tm", "lat"), None, None, None, None, None),
        check_vma=False,
    )
```

time: 190 us -> 189 us (level)
  blocking collectives: 29.9 us -> 52.6 us
  waiting for transfers between devices: 36.5 us -> 28.5 us
  local copies, waits for them, and re-layouts: 9.44 us -> 3.79 us
  Pallas kernels: 91.8 us -> 86.7 us
  starting transfers between devices: 17.8 us -> 13.2 us
    all_to_all x1, blocking collectives: 29.9 us -> 52.6 us  [shards(): lax.all_to_all(packed, ('tm', 'lat'), split_axis=0, concat_axis=0, tiled=...]
    all_to_all x3 -> x2, waiting for transfers between devices: 36.5 us -> 28.5 us  [shards(): lax.all_to_all(packed, ('tm', 'lat'), split_axis=0, concat_axis=0, tiled=...]
    pallas_call x10 -> x8, Pallas kernels: 91.8 us -> 86.7 us  [the longest x3 54.2 us: couple(): pl.pallas_call(body, grid_spec=pltpu.PrefetchScalarGridSpec(num_scalar_pr...]
    all_to_all x3 -> x2, starting transfers between devices: 15.5 us -> 10.9 us  [shards(): lax.all_to_all(packed, ('tm', 'lat'), split_axis=0, concat_axis=0, tiled=...]
    another operation x11 -> x0, local copies, waits for them, and re-layouts: 2.06 us -> none  [the longest x3 1.03 us: phase_turns(): return jnp.tile(turns, (1, 1, 4, 1))]
    unnamed x14 -> x13, local copies, waits for them, and re-layouts: 4.34 us -> 2.64 us
  transfers between devices with their start and end apart: 4 -> 3, of which waited for: 2 -> 2; matrix products, arithmetic and copies ran while one was open for 5% -> 2% of each run, Pallas kernels for 36% -> 21%
where the time goes in v2:
time: 189 us; the launch traced here: 186 us
  Pallas kernels  86.7 us (46%)
  blocking collectives  52.6 us (28%)
  waiting for transfers between devices  28.5 us (15%)
  starting transfers between devices  13.2 us (7%)
  local copies, waits for them, and re-layouts  3.79 us (2%)
    pallas_call x3, Pallas kernels, couple(): pl.pallas_call(body, grid_spec=pltpu.PrefetchScalarGridSpec(num_scalar_pr...  54.2 us
    all_to_all x1, blocking collectives, shards(): lax.all_to_all(packed, ('tm', 'lat'), split_axis=0, concat_axis=0, tiled=...  52.6 us
    all_to_all x2, waiting for transfers between devices, shards(): lax.all_to_all(packed, ('tm', 'lat'), split_axis=0, concat_axis=0, tiled=...  28.5 us
    pallas_call x2, Pallas kernels, azimuthal_transform(): pl.pallas_call(functools.partial(azimuthal_kernel, steps, count), in_spec...  18 us
    pallas_call x3, Pallas kernels, legendre(): pl.pallas_call(functools.partial(legendre_kernel, groups, first), grid=(o...  14.6 us
    all_to_all x2, starting transfers between devices, shards(): lax.all_to_all(packed, ('tm', 'lat'), split_axis=0, concat_axis=0, tiled=...  10.9 us
  transfers between devices with their start and end apart: 3, of which 2 were waited for; matrix products, arithmetic and copies ran while one was open for 2% of the time, Pallas kernels for 21%

profile of v2, /device:TPU:7, one launch (start us, length us, event | category | flops | bytes accessed | tf_op | source)
XLA Modules:
  0.0 185.8 jit_solution(1172976529804831325)
XLA Ops:
  0.0 0.0 copy-start
  0.0 10.3 %shard_map.127 = (bf16[96,32,2,128]{3,2,1,0:T(2,128)(2,1)}, bf16[32,32,2,128]{3,2,1,0:T(2,128)(2,1)}) custom-call(bf16[192,1024]{1,0:T(8,128)(2,1)} %constant.75.refs_0_, bf16[64,1024]{1,0:T(8,128)(2,1)} %constant.76.refs_1_, bf16[2,32,64,1024]{3,2,1,0:T(8,128)(2,1)} %bitcast.12), custom_call_target="tpu_custom_call" | custom-call | flops 2147483648 | bytes 8388608 | tf_op jit(solution)/shard_map/pallas_call | solution.py:88
  10.3 6.4 %all-to-all-start.1 = ((bf16[32,64,128]{2,1,0:T(8,128)(2,1)}), bf16[32,64,128]{2,1,0:T(8,128)(2,1)S(1)}, u32[]{:S(2)}, u32[]{:S(2)}) async-start(bf16[32,64,128]{2,1,0:T(8,128)(2,1)} %bitcast.18), calls=%async_computation.1 | async-start | bytes 1048576 | tf_op jit(solution)/shard_map/all_to_all | solution.py:326
  16.6 7.7 %shard_map.130 = bf16[128,32,2,128]{3,2,1,0:T(2,128)(2,1)} custom-call(bf16[256,1024]{1,0:T(8,128)(2,1)} %constant.77.refs_0_, bf16[2,32,64,1024]{3,2,1,0:T(8,128)(2,1)} %bitcast.13), custom_call_target="tpu_custom_call" | custom-call | flops 2147483648 | bytes 8388608 | tf_op jit(solution)/shard_map/pallas_call | solution.py:88
  24.4 6.5 %all-to-all-done.1 = bf16[32,64,128]{2,1,0:T(8,128)(2,1)S(1)} async-done(((bf16[32,64,128]{2,1,0:T(8,128)(2,1)}), bf16[32,64,128]{2,1,0:T(8,128)(2,1)S(1)}, u32[]{:S(2)}, u32[]{:S(2)}) %all-to-all-start.1) | async-done | bytes 524320 | tf_op jit(solution)/shard_map/all_to_all | solution.py:326
  30.8 0.0 copy-start.3
  30.8 52.6 %all_to_all.15 = bf16[32,256,128]{2,1,0:T(8,128)(2,1)} all-to-all(bf16[32,256,128]{2,1,0:T(8,128)(2,1)} %bitcast.15), channel_id=1, replica_groups=mesh['tm'=4,'lat'=8] {'tm','lat'}, dimensions={0} | all-to-all | bytes 4194304 | tf_op jit(solution)/shard_map/all_to_all | solution.py:326
  83.4 0.0 copy-done.3
  83.4 0.0 copy-start.4
  83.4 0.0 copy-start.5
  83.4 4.5 %all-to-all-start = ((bf16[32,192,128]{2,1,0:T(8,128)(2,1)}), bf16[32,192,128]{2,1,0:T(8,128)(2,1)S(1)}, u32[]{:S(2)}, u32[]{:S(2)}) async-start(bf16[32,192,128]{2,1,0:T(8,128)(2,1)} %bitcast.1), calls=%async_computation | async-start | bytes 3145728 | tf_op jit(solution)/shard_map/all_to_all | solution.py:326
  88.0 0.0 copy-done
  88.0 0.1 constant_dynamic-slice_fusion
  88.1 0.7 copy.18.bounds_ref
  88.8 0.0 copy-done.4
  88.8 0.0 copy-done.5
  88.8 0.1 cosine_multiply_fusion
  88.9 0.1 broadcast_select_fusion.2
  89.0 0.7 broadcast_select_fusion.refs_0_
  89.7 2.9 %shard_map.129.refs_3_ = bf16[1,512,256]{2,1,0:T(8,128)(2,1)} custom-call(s32[8,2]{1,0:T(8,128)} %copy.18.bounds_ref, bf16[4,8,1,64,128]{4,3,2,1,0:T(8,128)(2,1)} %bitcast.17, bf16[8,512,256]{2,1,0:T(8,128)(2,1)} %projection_ref.5, bf16[256,256]{1,0:T(8,128)(2,1)} %constant.70.clone.sort_ref), custom_call_target="tpu_custom_call" | custom-call | flops 268435456 | bytes 524288 | tf_op jit(solution)/shard_map/pallas_call | solution.py:147
  92.7 6.4 %shard_map.131.refs_2_ = bf16[4,512,256]{2,1,0:T(8,128)(2,1)} custom-call(s32[8,2]{1,0:T(8,128)} %copy.18.bounds_ref, bf16[4,8,4,64,128]{4,3,2,1,0:T(8,128)(2,1)} %bitcast.14, bf16[8,512,256]{2,1,0:T(8,128)(2,1)} %projection_ref.5, bf16[256,256]{1,0:T(8,128)(2,1)} %constant.70.clone.sort_ref), custom_call_target="tpu_custom_call" | custom-call | flops 1073741824 | bytes 2097152 | tf_op jit(solution)/shard_map/pallas_call | solution.py:147
  99.0 1.1 slice.4
  100.1 2.3 %collective-permute-start = (bf16[2,512,256]{2,1,0:T(8,128)(2,1)S(1)}, bf16[2,512,256]{2,1,0:T(8,128)(2,1)S(1)}, u32[]{:S(2)}, u32[]{:S(2)}) collective-permute-start(bf16[2,512,256]{2,1,0:T(8,128)(2,1)S(1)} %slice.4), channel_id=1, source_target_pairs={{1,0},{2,1},{3,2},{4,3},{5,4},{6,5},{7,6},{8,7},{9,8},{10,9},{11,1... | collective-permute-start | bytes 1572872 | tf_op jit(solution)/shard_map/ppermute | solution.py:25
  102.4 22.0 %all-to-all-done = bf16[32,192,128]{2,1,0:T(8,128)(2,1)S(1)} async-done(((bf16[32,192,128]{2,1,0:T(8,128)(2,1)}), bf16[32,192,128]{2,1,0:T(8,128)(2,1)S(1)}, u32[]{:S(2)}, u32[]{:S(2)}) %all-to-all-start) | async-done | bytes 1572896 | tf_op jit(solution)/shard_map/all_to_all | solution.py:326
  124.5 0.0 copy-start.1
  124.5 1.1 copy-done.1
  125.6 5.3 %shard_map.128.refs_3_.refs_2_ = bf16[3,512,256]{2,1,0:T(8,128)(2,1)} custom-call(s32[8,2]{1,0:T(8,128)} %copy.18.bounds_ref, bf16[4,8,3,64,128]{4,3,2,1,0:T(8,128)(2,1)} %bitcast.16, bf16[8,512,256]{2,1,0:T(8,128)(2,1)} %projection_ref.5, bf16[256,256]{1,0:T(8,128)(2,1)} %constant.70.clone.sort_ref), custom_call_target="tpu_custom_call" | custom-call | flops 805306368 | bytes 1572864 | tf_op jit(solution)/shard_map/pallas_call | solution.py:147
  130.9 16.9 %shard_map.132.refs_5_ = bf16[8,2,8,1024,128]{4,3,2,1,0:T(8,128)(2,1)} custom-call(s32[10]{0:T(128)} %constant.71.clone.places_ref, f32[8,2,8,256]{3,2,1,0:T(8,128)} %broadcast_select_fusion.refs_0_, bf16[512,256]{1,0:T(8,128)(2,1)} %constant.69.clone.refs_1_, bf16[4,512,256]{2,1,0:T(8,128)(2,1)} %shard_map.131.refs_2_), custom_call_target="tpu_custom_call" | custom-call | flops 5368709120 | bytes 10485760 | tf_op jit(solution)/shard_map/pallas_call | solution.py:238
  147.8 0.0 collective-permute-done.refs_4_
  147.8 0.0 copy-start.2
  147.8 0.8 copy-done.2
  148.6 23.1 %shard_map.133.refs_5_ = bf16[8,2,8,1024,128]{4,3,2,1,0:T(8,128)(2,1)} custom-call(s32[14]{0:T(128)} %constant.72.clone.places_ref, f32[8,2,8,256]{3,2,1,0:T(8,128)} %broadcast_select_fusion.refs_0_, bf16[512,256]{1,0:T(8,128)(2,1)} %constant.69.clone.refs_1_, bf16[4,512,256]{2,1,0:T(8,128)(2,1)} %shard_map.131.refs_2_, ...), custom_call_target="tpu_custom_call", output_to_operand_aliasing={{}: (6, {})} | custom-call | flops 7516192768 | bytes 14680064 | tf_op jit(solution)/shard_map/pallas_call | solution.py:238
  171.7 14.2 %shard_map.134 = bf16[8,2,8,1024,128]{4,3,2,1,0:T(8,128)(2,1)} custom-call(s32[8]{0:T(128)} %constant.73.clone.places_ref, f32[8,2,8,256]{3,2,1,0:T(8,128)} %broadcast_select_fusion.refs_0_, bf16[512,256]{1,0:T(8,128)(2,1)} %constant.69.clone.refs_1_, bf16[3,512,256]{2,1,0:T(8,128)(2,1)} %shard_map.128.refs_3_.refs_2_, ...), custom_call_target="tpu_custom_call", output_to_operand_aliasing={{}: (6, {})} | custom-call | flops 4294967296 | bytes 8388608 | tf_op jit(solution)/shard_map/pallas_call | solution.py:238
  (2 shorter events, 0.0 us)
Async XLA Ops:
  0.0 88.0 %copy-start = (s32[256,2]{0,1:T(2,128)S(1)}, s32[256,2]{0,1:T(2,128)}, u32[]{:S(2)}) copy-start(s32[256,2]{0,1:T(2,128)} %param.15) | copy-start | bytes 6148
  10.3 20.6 %all-to-all-start.1 = ((bf16[32,64,128]{2,1,0:T(8,128)(2,1)}), bf16[32,64,128]{2,1,0:T(8,128)(2,1)S(1)}, u32[]{:S(2)}, u32[]{:S(2)}) async-start(bf16[32,64,128]{2,1,0:T(8,128)(2,1)} %bitcast.18), calls=%async_computation.1 | async-start | bytes 1048576 | tf_op jit(solution)/shard_map/all_to_all | solution.py:326
  30.8 52.6 %copy-start.3 = (bf16[32,64,128]{2,1,0:T(8,128)(2,1)}, bf16[32,64,128]{2,1,0:T(8,128)(2,1)S(1)}, u32[]{:S(2)}) copy-start(bf16[32,64,128]{2,1,0:T(8,128)(2,1)S(1)} %all-to-all-done.1) | copy-start | bytes 1572868
  83.4 5.3 %copy-start.4 = (s32[256]{0:T(256)S(1)}, s32[256]{0:T(256)}, u32[]{:S(2)}) copy-start(s32[256]{0:T(256)} %constant.68.clone) | copy-start | bytes 3076
  83.4 5.3 %copy-start.5 = (s32[8]{0:T(128)S(1)}, s32[8]{0:T(128)}, u32[]{:S(2)}) copy-start(s32[8]{0:T(128)} %param.16) | copy-start | bytes 100
  83.4 41.0 %all-to-all-start = ((bf16[32,192,128]{2,1,0:T(8,128)(2,1)}), bf16[32,192,128]{2,1,0:T(8,128)(2,1)S(1)}, u32[]{:S(2)}, u32[]{:S(2)}) async-start(bf16[32,192,128]{2,1,0:T(8,128)(2,1)} %bitcast.1), calls=%async_computation | async-start | bytes 3145728 | tf_op jit(solution)/shard_map/all_to_all | solution.py:326
  100.1 47.7 %collective-permute-start = (bf16[2,512,256]{2,1,0:T(8,128)(2,1)S(1)}, bf16[2,512,256]{2,1,0:T(8,128)(2,1)S(1)}, u32[]{:S(2)}, u32[]{:S(2)}) collective-permute-start(bf16[2,512,256]{2,1,0:T(8,128)(2,1)S(1)} %slice.4), channel_id=1, source_target_pairs={{1,0},{2,1},{3,2},{4,3},{5,4},{6,5},{7,6},{8,7},{9,8},{10,9},{11,1... | collective-permute-start | bytes 1572872 | tf_op jit(solution)/shard_map/ppermute | solution.py:25
  124.5 1.1 copy-start.1
  147.8 0.8 copy-start.2

commit v3 on v2

v3 whole, which is shorter than its diff:
```python
import functools
import math
from typing import NamedTuple

import jax
import jax.numpy as jnp
import numpy as np
from jax import lax
from jax.experimental import pallas as pl
from jax.experimental.pallas import tpu as pltpu
from jax.sharding import PartitionSpec as P

LANES = 128
VMEM_LIMIT = 60 * 1024 * 1024


def chunk_sizes(orders):
    if orders < 6:
        return [orders]
    return [4, 2, 2]


def shifted(block, axis, distance):
    devices = range(lax.axis_size(axis))
    route = [(i - distance, i) for i in devices if i - distance in devices]
    return lax.ppermute(block, axis, route)


def longitude_rows(lon_count, order_ids):
    phase = np.asarray(order_ids, np.int64)[:, None] * np.arange(lon_count)[None, :] % lon_count
    angle = phase * (2.0 * math.pi / lon_count)
    factor = 1.0 / math.sqrt(lon_count)
    table = np.stack([np.cos(angle) * factor, -np.sin(angle) * factor], axis=1)
    return jnp.asarray(table.reshape(-1, lon_count).astype(np.float32)).astype(jnp.bfloat16)


def azimuthal_kernel(steps, count, *refs):
    table_refs, frames_ref, out_refs = refs[:count], refs[count], refs[count + 1 : 2 * count + 1]
    held, stages = refs[2 * count + 1], refs[2 * count + 2 : 3 * count + 2]
    in_sem, out_sem = refs[-2:]
    groups, times, lat_rows, lon_count = frames_ref.shape
    pieces = times // steps
    width = groups * lat_rows

    def load(i):
        span = pl.ds(i * steps, steps)
        return pltpu.make_async_copy(frames_ref.at[:, span], held.at[:, span], in_sem.at[i])

    def save(c, i):
        span = pl.ds(i * steps, steps)
        return pltpu.make_async_copy(
            stages[c].at[:, span], out_refs[c].at[:, span], out_sem.at[c, i]
        )

    for i in range(pieces):
        load(i).start()

    def piece(i, carry):
        load(i).wait()
        for pair in range(0, steps, 2):
            spans = range(pair, min(pair + 2, steps))
            block = jnp.concatenate(
                [held[:, i * steps + g].reshape(width, lon_count) for g in spans], axis=0
            )
            for c in range(count):
                value = lax.dot_general(
                    table_refs[c][...],
                    block,
                    (((1,), (1,)), ((), ())),
                    preferred_element_type=jnp.float32,
                ).astype(jnp.bfloat16)
                for n, g in enumerate(spans):
                    part = value[:, n * width : (n + 1) * width]
                    stages[c][:, i * steps + g] = part.reshape(part.shape[0] // 2, 2, width)
        for c in range(count):
            save(c, i).start()
        return carry

    lax.fori_loop(0, pieces, piece, 0)
    for c in range(count):
        for i in range(pieces):
            save(c, i).wait()


def azimuthal_transform(tables, frames, steps):
    count = len(tables)
    groups, times, lat_rows, _ = frames.shape
    shapes = [(t.shape[0] // 2, times, 2, groups * lat_rows) for t in tables]
    return pl.pallas_call(
        functools.partial(azimuthal_kernel, steps, count),
        in_specs=[pl.BlockSpec(memory_space=pltpu.VMEM)] * count
        + [pl.BlockSpec(memory_space=pl.ANY)],
        out_specs=[pl.BlockSpec(memory_space=pl.ANY)] * count,
        out_shape=[jax.ShapeDtypeStruct(s, jnp.bfloat16) for s in shapes],
        scratch_shapes=[pltpu.VMEM(frames.shape, jnp.bfloat16)]
        + [pltpu.VMEM(s, jnp.bfloat16) for s in shapes]
        + [
            pltpu.SemaphoreType.DMA((times // steps,)),
            pltpu.SemaphoreType.DMA((count, times // steps)),
        ],
        compiler_params=pltpu.CompilerParams(vmem_limit_bytes=VMEM_LIMIT),
        cost_estimate=pl.CostEstimate(
            flops=2 * sum(t.shape[0] for t in tables) * frames.size,
            bytes_accessed=2 * frames.size,
            transcendentals=0,
        ),
    )(*tables, frames)


def joined(ref, *index):
    part = ref.at[index] if index else ref
    return jnp.concatenate([part[n] for n in range(part.shape[0])], axis=1)


def legendre_kernel(groups, first, bounds_ref, wire_ref, projection_ref, sort_ref, twice_ref, *rest):
    harmonic_ref, doubled_ref, wide = rest
    _, lat_groups, _, rows, lanes = wire_ref.shape
    degrees = projection_ref.shape[-1]
    tiles = degrees // LANES
    lat_rows = lanes // groups
    order = pl.program_id(0)

    @pl.when(order == 0)
    def _():
        wide[...] = jnp.zeros_like(wide)

    for a in range(lat_groups):
        band = projection_ref[0, a * lat_rows : (a + 1) * lat_rows, :]
        for g in range(groups):
            start = a * lanes + g * lat_rows
            for n in range(tiles):
                wide[g * tiles + n, start : start + lat_rows] = band[:, n * LANES : (n + 1) * LANES]
    tall = wire_ref.shape[0] * rows
    half = tall // 2
    left = jnp.concatenate(
        [wire_ref[:, a, 0].reshape(tall, lanes) for a in range(lat_groups)], axis=1
    )
    summed = jnp.dot(left, joined(wide), preferred_element_type=jnp.float32)
    lane = lax.broadcasted_iota(jnp.int32, (tall, groups * degrees), 1) % degrees
    low, high = bounds_ref[order + first, 0], bounds_ref[order + first, 1]
    kept = jnp.where((lane >= low) & (lane < high), summed, 0.0).astype(jnp.bfloat16)
    parted = jnp.dot(joined(sort_ref), kept, preferred_element_type=jnp.float32)
    parted = parted.astype(jnp.bfloat16)
    for q in range(2):
        for g in range(groups):
            start = (q * groups + g) * half
            for n in range(tiles):
                column = (g * tiles + n) * LANES
                harmonic_ref[0, n, start : start + half] = parted[
                    q * half : (q + 1) * half, column : column + LANES
                ]
    real, imaginary = (
        jnp.concatenate(
            [
                parted[q * half : (q + 1) * half, g * degrees : (g + 1) * degrees]
                for g in range(groups)
            ],
            axis=0,
        )
        for q in range(2)
    )
    length = groups * half
    for q, pair in enumerate(((real, -imaginary), (imaginary, real))):
        block = lax.dot_general(
            joined(twice_ref),
            jnp.concatenate(pair, axis=1),
            (((1,), (1,)), ((), ())),
            preferred_element_type=jnp.float32,
        ).astype(jnp.bfloat16)
        for n in range(length // LANES):
            doubled_ref[0, q * length // LANES + n] = block[:, n * LANES : (n + 1) * LANES]


def legendre(groups, first, bounds, wire, projection, sort, twice):
    tm_count, lat_groups, orders, rows, lanes = wire.shape
    _, lat_total, degrees = projection.shape
    total = groups * tm_count * rows
    harmonic = (degrees // LANES, total, LANES)
    doubled = (total // LANES, 2 * degrees, LANES)
    return pl.pallas_call(
        functools.partial(legendre_kernel, groups, first),
        grid=(orders,),
        in_specs=[
            pl.BlockSpec(memory_space=pltpu.SMEM),
            pl.BlockSpec((tm_count, lat_groups, 1, rows, lanes), lambda o: (0, 0, o, 0, 0)),
            pl.BlockSpec((1, lat_total, degrees), lambda o: (o + first, 0, 0)),
            pl.BlockSpec(sort.shape, lambda o: (0, 0, 0)),
            pl.BlockSpec(twice.shape, lambda o: (0, 0, 0)),
        ],
        out_specs=[
            pl.BlockSpec((1,) + harmonic, lambda o: (o, 0, 0, 0)),
            pl.BlockSpec((1,) + doubled, lambda o: (o, 0, 0, 0)),
        ],
        out_shape=[
            jax.ShapeDtypeStruct((orders,) + harmonic, jnp.bfloat16),
            jax.ShapeDtypeStruct((orders,) + doubled, jnp.bfloat16),
        ],
        scratch_shapes=[
            pltpu.VMEM((groups * degrees // LANES, lat_groups * lanes, LANES), jnp.bfloat16)
        ],
        compiler_params=pltpu.CompilerParams(vmem_limit_bytes=VMEM_LIMIT),
        cost_estimate=pl.CostEstimate(
            flops=2 * wire.size * groups * degrees,
            bytes_accessed=2 * wire.size,
            transcendentals=0,
        ),
    )(bounds, wire, projection, sort, twice)


def couple_kernel(jobs, own_count, partner_count, plan_ref, turn_ref, *rest):
    owns, partners = rest[:own_count], rest[own_count : own_count + partner_count]
    out_ref, own, raw, partner, turns, turned_a, turned_b, stage, own_sem, raw_sem, out_sem = rest[
        -11:
    ]
    job = pl.program_id(0)
    tiles, total, _ = partner.shape
    degrees = tiles * LANES
    half = total // 2
    tall = 2 * degrees
    offsets = turns.shape[0]

    def fetches(n):
        array, index = jobs[n].partner
        copies = [
            pltpu.make_async_copy(partners[array].at[index], raw.at[n % 2], raw_sem.at[n % 2])
        ]
        for (array, index), buffer in jobs[n].fetched:
            copies.append(
                pltpu.make_async_copy(owns[array].at[index], own.at[buffer], own_sem.at[buffer])
            )
        return copies

    def saves(n):
        return [
            pltpu.make_async_copy(
                stage.at[n % 2, i], out_ref.at[place[0], place[1]], out_sem.at[n % 2, i]
            )
            for i, place in enumerate(jobs[n].places)
        ]

    @pl.when(job == 0)
    def _():
        for copy in fetches(0):
            copy.start()
        for k in range(offsets):
            for n in range(2):
                column = turn_ref[:, 2 * k + n : 2 * k + n + 1]
                turns[k, n] = jnp.broadcast_to(column, (half, LANES))

    for n in range(len(jobs)):

        @pl.when(job == n)
        def _():
            if n + 1 < len(jobs):
                for copy in fetches(n + 1):
                    copy.start()
            for copy in fetches(n):
                copy.wait()
            if n >= 2:
                for copy in saves(n - 2):
                    copy.wait()

    slot = job % 2
    for n in range(tiles):
        partner[n] = raw[slot, n].astype(jnp.float32)

    def turn(k, target):
        cosine, sine = turns[k, 0], turns[k, 1]
        for n in range(tiles):
            x, y = partner[n, :half], partner[n, half:]
            target[n, :half] = (x * cosine + y * sine).astype(jnp.bfloat16)
            target[n, half:] = (y * cosine - x * sine).astype(jnp.bfloat16)

    pair = lax.broadcasted_iota(jnp.int32, (tall // 8, 8, LANES), 1) % 4 < 2

    def products(count):
        turn(0, turned_a)
        for k in range(offsets):
            now, later = (turned_a, turned_b) if k % 2 == 0 else (turned_b, turned_a)
            if k + 1 < offsets:
                turn(k + 1, later)
            for i in range(count):
                left = joined(own, plan_ref[3 * job + 1 + i])
                product = jnp.dot(left, joined(now), preferred_element_type=jnp.float32)
                for n in range(tiles // 2):
                    a, b = (
                        product[:, (2 * n + t) * LANES : (2 * n + t + 1) * LANES].reshape(
                            tall // 8, 8, LANES
                        )
                        for t in range(2)
                    )
                    upper = jnp.where(pair, a, pltpu.roll(b, 2, 1))
                    lower = jnp.where(pair, pltpu.roll(a, 6, 1), b)
                    mixed = jnp.stack([upper, lower], axis=1).reshape(2 * tall, LANES)
                    stage[slot, i, k] = mixed.astype(jnp.bfloat16)

    counts = sorted({len(one.places) for one in jobs})
    for count in counts:
        if len(counts) == 1:
            products(count)
        else:
            pl.when(plan_ref[3 * job] == count)(functools.partial(products, count))

    for n in range(len(jobs)):

        @pl.when(job == n)
        def _():
            for copy in saves(n):
                copy.start()
            if n == len(jobs) - 1:
                for m in range(max(n - 1, 0), n + 1):
                    for copy in saves(m):
                        copy.wait()


class Job(NamedTuple):
    partner: tuple
    fetched: tuple
    buffers: tuple
    places: tuple


def plan_jobs(pairs, spot, own_used, partner_used):
    held, jobs = [None] * 3, []
    for p in sorted({o + 1 + s for o, s in pairs}):
        places = tuple((o, s) for o, s in sorted(pairs, reverse=True) if o + 1 + s == p)
        wanted = [o for o, _ in places]
        busy = [] if not jobs else list(jobs[-1].buffers)
        fetched = []
        for o in wanted:
            if o not in held:
                buffer = next(
                    n for n in range(3) if n not in busy and held[n] not in wanted
                )
                held[buffer] = o
                array, index = spot[o]
                fetched.append(((own_used.index(array), index), buffer))
        array, index = spot[p]
        jobs.append(
            Job(
                (partner_used.index(array), index),
                tuple(fetched),
                tuple(held.index(o) for o in wanted),
                places,
            )
        )
    return jobs


def couple(turn, offsets, doubled, harmonics, pairs, spot, out, shape):
    own_used = sorted({spot[o][0] for o, _ in pairs})
    partner_used = sorted({spot[o + 1 + s][0] for o, s in pairs})
    owns, partners = [doubled[a] for a in own_used], [harmonics[a] for a in partner_used]
    jobs = plan_jobs(pairs, spot, own_used, partner_used)
    _, tiles, total, _ = partners[0].shape
    tall = 2 * tiles * LANES
    plan = [[len(one.places)] + (list(one.buffers) + [0])[:2] for one in jobs]
    operands = [turn] + owns + partners
    specs = [pl.BlockSpec(turn.shape, lambda j, plan_ref: (0, 0))]
    specs += [pl.BlockSpec(memory_space=pl.ANY)] * len(owns + partners)
    aliases = {}
    if out is not None:
        aliases = {len(operands) + 1: 0}
        operands.append(out)
        specs.append(pl.BlockSpec(memory_space=pl.ANY))
    return pl.pallas_call(
        functools.partial(couple_kernel, jobs, len(owns), len(partners)),
        grid_spec=pltpu.PrefetchScalarGridSpec(
            num_scalar_prefetch=1,
            grid=(len(jobs),),
            in_specs=specs,
            out_specs=pl.BlockSpec(memory_space=pl.ANY),
            scratch_shapes=[
                pltpu.VMEM((3,) + owns[0].shape[1:], jnp.bfloat16),
                pltpu.VMEM((2, tiles, total, LANES), jnp.bfloat16),
                pltpu.VMEM((tiles, total, LANES), jnp.float32),
                pltpu.VMEM((offsets, 2, total // 2, LANES), jnp.float32),
                pltpu.VMEM((tiles, total, LANES), jnp.bfloat16),
                pltpu.VMEM((tiles, total, LANES), jnp.bfloat16),
                pltpu.VMEM((2, 2, offsets, 2 * tall, LANES), jnp.bfloat16),
                pltpu.SemaphoreType.DMA((3,)),
                pltpu.SemaphoreType.DMA((2,)),
                pltpu.SemaphoreType.DMA((2, 2)),
            ],
        ),
        out_shape=shape,
        input_output_aliases=aliases,
        compiler_params=pltpu.CompilerParams(vmem_limit_bytes=VMEM_LIMIT),
        cost_estimate=pl.CostEstimate(
            flops=2 * len(pairs) * offsets * total * tall * tiles * LANES,
            bytes_accessed=2 * len(pairs) * offsets * tall * tiles * LANES,
            transcendentals=0,
        ),
    )(jnp.asarray(np.asarray(plan, np.int32).reshape(-1)), *operands)


def tiled_one_hot(columns, width):
    table = np.asarray(columns)[:, None] == np.arange(width)[None, :]
    tiles = table.reshape(len(columns), width // LANES, LANES).swapaxes(0, 1)
    return jnp.asarray(tiles, jnp.bfloat16)


def phase_turns(offsets, times, frame_count):
    lane_offsets = jnp.pad(jnp.repeat(offsets, 2), (0, LANES - 2 * offsets.shape[0]))
    phase = times[:, None] * lane_offsets[None, :] % frame_count
    angle = phase.astype(jnp.float32) * (2.0 * math.pi / frame_count)
    even = jnp.arange(LANES, dtype=jnp.int32)[None, :] % 2 == 0
    return jnp.where(even, jnp.cos(angle), jnp.sin(angle)) * (1.0 / math.sqrt(frame_count))


def shards(frames, projection, degree_range, offsets):
    frame_rows, lat_rows, lon_count = frames.shape
    orders, _, degrees = projection.shape
    tm_count, lat_groups = lax.axis_size("tm"), lax.axis_size("lat")
    devices = tm_count * lat_groups
    frame_count = frame_rows * tm_count
    groups = LANES // lat_rows
    times = frame_rows // groups
    steps = min(8, times)
    sizes = chunk_sizes(orders)
    starts = [sum(sizes[:c]) for c in range(len(sizes))]

    ids = np.arange(devices * orders).reshape(devices, orders)
    tables = [
        longitude_rows(lon_count, ids[:, a : a + n].reshape(-1)) for a, n in zip(starts, sizes)
    ]
    grouped = frames.reshape(groups, times, lat_rows, lon_count)
    sent = list(azimuthal_transform(tables[:1], grouped, steps))
    if len(sizes) > 1:
        sent += list(azimuthal_transform(tables[1:], grouped, steps))

    rank = lax.axis_index("tm") * lat_groups + lax.axis_index("lat")
    bounds = lax.dynamic_slice_in_dim(degree_range, rank * orders, orders, 0)
    time_ids = (
        np.arange(tm_count)[None, :, None] * frame_rows
        + np.arange(groups)[:, None, None] * times
        + np.arange(times)[None, None, :]
    ).reshape(-1)
    turn = phase_turns(offsets, jnp.asarray(time_ids, jnp.int32), frame_count)
    row = np.arange(2 * degrees)
    degree_of = row // 8 * 4 + np.array([0, 2, 1, 3])[row % 8 // 2]
    column_of = degree_of + row % 2 * degrees
    twice = tiled_one_hot(column_of, 2 * degrees)
    tall = tm_count * times * 2
    source = np.arange(tall) % (tall // 2) * 2 + np.arange(tall) // (tall // 2)
    sort = tiled_one_hot(source, tall)

    shape = jax.ShapeDtypeStruct(
        (orders, 2, offsets.shape[0], 2 * degrees * degrees // LANES, LANES), jnp.bfloat16
    )
    spot = [(c, n) for c, size in enumerate(sizes) for n in range(size)]
    spot += [(len(sizes), n) for n in range(2)]
    harmonics = [None] * (len(sizes) + 1)
    doubled = [None] * len(sizes)
    done = set()
    out = None
    for c, (start, size) in enumerate(zip(starts, sizes)):
        packed = sent[c].reshape(devices, size * times * 2, LANES)
        moved = lax.all_to_all(packed, ("tm", "lat"), split_axis=0, concat_axis=0, tiled=True)
        wire = moved.reshape(tm_count, lat_groups, size, times * 2, LANES)
        harmonics[c], doubled[c] = legendre(groups, start, bounds, wire, projection, sort, twice)
        if c == 0:
            harmonics[-1] = shifted(harmonics[0][:2], ("tm", "lat"), -1)
        end = start + size
        ready = [
            (o, s)
            for o in range(end)
            for s in range(2)
            if (o, s) not in done
            and (o + 1 + s < end or (o + 1 + s >= orders and (c > 0 or c == len(sizes) - 1)))
        ]
        done.update(ready)
        if ready:
            out = couple(
                turn, offsets.shape[0], doubled, harmonics, ready, spot, out, shape
            )
    out = out.reshape(
        orders, 2, offsets.shape[0], degrees, degrees // LANES, 2, LANES
    )
    return jnp.swapaxes(out, 4, 5).reshape(orders, 2, offsets.shape[0], degrees, 2, degrees)


def solution(mesh):
    return jax.shard_map(
        shards,
        mesh=mesh,
        in_specs=(P("tm", "lat", None), P(("tm", "lat"), None, None), P(), P()),
        out_specs=P(("tm", "lat"), None, None, None, None, None),
        check_vma=False,
    )
```

time: 189 us -> 176 us (0.931)
  waiting for transfers between devices: 28.5 us -> 54.5 us
  blocking collectives: 52.6 us -> 31.7 us
  Pallas kernels: 86.7 us -> 70.1 us
    all_to_all x2, waiting for transfers between devices: 28.5 us -> 54.5 us  [shards(): lax.all_to_all(packed, ('tm', 'lat'), split_axis=0, concat_axis=0, tiled=...]
    all_to_all x1, blocking collectives: 52.6 us -> 31.7 us  [shards(): lax.all_to_all(packed, ('tm', 'lat'), split_axis=0, concat_axis=0, tiled=...]
    pallas_call x3, Pallas kernels: 54.2 us -> 36.5 us  [couple(): pl.pallas_call(functools.partial(couple_kernel, jobs, len(owns), len(part...]
  transfers between devices with their start and end apart: 3 -> 3, of which waited for: 2 -> 2; matrix products, arithmetic and copies ran while one was open for 2% -> 1% of each run, Pallas kernels for 21% -> 22%
where the time goes in v3:
time: 176 us; the launch traced here: 174 us
  Pallas kernels  70.1 us (40%)
  waiting for transfers between devices  54.5 us (31%)
  blocking collectives  31.7 us (18%)
  starting transfers between devices  12.2 us (7%)
  local copies, waits for them, and re-layouts  4.1 us (2%)
    all_to_all x2, waiting for transfers between devices, shards(): lax.all_to_all(packed, ('tm', 'lat'), split_axis=0, concat_axis=0, tiled=...  54.5 us
    pallas_call x3, Pallas kernels, couple(): pl.pallas_call(functools.partial(couple_kernel, jobs, len(owns), len(part...  36.5 us
    all_to_all x1, blocking collectives, shards(): lax.all_to_all(packed, ('tm', 'lat'), split_axis=0, concat_axis=0, tiled=...  31.7 us
    pallas_call x2, Pallas kernels, azimuthal_transform(): pl.pallas_call(functools.partial(azimuthal_kernel, steps, count), in_spec...  17.6 us
    pallas_call x3, Pallas kernels, legendre(): pl.pallas_call(functools.partial(legendre_kernel, groups, first), grid=(o...  16 us
    all_to_all x2, starting transfers between devices, shards(): lax.all_to_all(packed, ('tm', 'lat'), split_axis=0, concat_axis=0, tiled=...  9.14 us
  transfers between devices with their start and end apart: 3, of which 2 were waited for; matrix products, arithmetic and copies ran while one was open for 1% of the time, Pallas kernels for 22%

profile of v3, /device:TPU:7, one launch (start us, length us, event | category | flops | bytes accessed | tf_op | source)
XLA Modules:
  0.0 174.2 jit_solution(397034606326944456)
XLA Ops:
  0.0 0.0 copy-start
  0.0 10.2 %shard_map.127 = (bf16[64,32,2,128]{3,2,1,0:T(2,128)(2,1)}, bf16[64,32,2,128]{3,2,1,0:T(2,128)(2,1)}) custom-call(bf16[128,1024]{1,0:T(8,128)(2,1)} %constant.76.refs_0_, bf16[128,1024]{1,0:T(8,128)(2,1)} %constant.77.refs_1_, bf16[2,32,64,1024]{3,2,1,0:T(8,128)(2,1)} %bitcast.12), custom_call_target="tpu_custom_call" | custom-call | flops 2147483648 | bytes 8388608 | tf_op jit(solution)/shard_map/pallas_call | solution.py:89
  10.2 31.7 %all_to_all.15 = bf16[32,128,128]{2,1,0:T(8,128)(2,1)} all-to-all(bf16[32,128,128]{2,1,0:T(8,128)(2,1)} %bitcast.19), channel_id=1, replica_groups=mesh['tm'=4,'lat'=8] {'tm','lat'}, dimensions={0} | all-to-all | bytes 2097152 | tf_op jit(solution)/shard_map/all_to_all | solution.py:459
  42.0 0.0 copy-start.5
  42.0 0.0 copy-start.4
  42.0 4.6 %all-to-all-start = ((bf16[32,128,128]{2,1,0:T(8,128)(2,1)}), bf16[32,128,128]{2,1,0:T(8,128)(2,1)S(1)}, u32[]{:S(2)}, u32[]{:S(2)}) async-start(bf16[32,128,128]{2,1,0:T(8,128)(2,1)} %bitcast.18), calls=%async_computation | async-start | bytes 2097152 | tf_op jit(solution)/shard_map/all_to_all | solution.py:459
  46.5 7.4 %shard_map.130 = bf16[128,32,2,128]{3,2,1,0:T(2,128)(2,1)} custom-call(bf16[256,1024]{1,0:T(8,128)(2,1)} %constant.78.refs_0_, bf16[2,32,64,1024]{3,2,1,0:T(8,128)(2,1)} %bitcast.13), custom_call_target="tpu_custom_call" | custom-call | flops 2147483648 | bytes 8388608 | tf_op jit(solution)/shard_map/pallas_call | solution.py:89
  53.9 17.9 %all-to-all-done = bf16[32,128,128]{2,1,0:T(8,128)(2,1)S(1)} async-done(((bf16[32,128,128]{2,1,0:T(8,128)(2,1)}), bf16[32,128,128]{2,1,0:T(8,128)(2,1)S(1)}, u32[]{:S(2)}, u32[]{:S(2)}) %all-to-all-start) | async-done | bytes 1048608 | tf_op jit(solution)/shard_map/all_to_all | solution.py:459
  71.8 0.0 copy-start.2
  71.8 4.6 %all-to-all-start.2 = ((bf16[32,256,128]{2,1,0:T(8,128)(2,1)}), bf16[32,256,128]{2,1,0:T(8,128)(2,1)S(1)}, u32[]{:S(2)}, u32[]{:S(2)}) async-start(bf16[32,256,128]{2,1,0:T(8,128)(2,1)} %bitcast.15), calls=%async_computation.2 | async-start | bytes 4194304 | tf_op jit(solution)/shard_map/all_to_all | solution.py:459
  76.4 0.0 copy-done
  76.4 0.1 constant_dynamic-slice_fusion
  76.5 0.7 copy.20.bounds_ref
  77.1 0.0 copy-done.5
  77.1 0.1 broadcast_in_dim.15
  77.2 0.1 reshape.49
  77.3 0.0 copy-done.4
  77.3 1.2 select_multiply_fusion.turn_ref
  78.6 0.0 copy-done.2
  78.6 4.6 %shard_map.128 = (bf16[2,2,512,128]{3,2,1,0:T(8,128)(2,1)}, bf16[2,4,512,128]{3,2,1,0:T(8,128)(2,1)}) custom-call(s32[8,2]{1,0:T(8,128)} %copy.20.bounds_ref, bf16[4,8,2,64,128]{4,3,2,1,0:T(8,128)(2,1)} %bitcast.17, bf16[8,512,256]{2,1,0:T(8,128)(2,1)} %projection_ref.5, bf16[2,256,128]{2,1,0:T(8,128)(2,1)} %constant.69.clone.sort_ref, ...), custom_call_target="tpu_custom_call" | custom-call | flops 536870912 | bytes 1048576 | tf_op jit(solution)/shard_map/pallas_call | solution.py:180
  83.1 4.5 %shard_map.129 = (bf16[2,2,512,128]{3,2,1,0:T(8,128)(2,1)}, bf16[2,4,512,128]{3,2,1,0:T(8,128)(2,1)}) custom-call(s32[8,2]{1,0:T(8,128)} %copy.20.bounds_ref, bf16[4,8,2,64,128]{4,3,2,1,0:T(8,128)(2,1)} %bitcast.16, bf16[8,512,256]{2,1,0:T(8,128)(2,1)} %projection_ref.5, bf16[2,256,128]{2,1,0:T(8,128)(2,1)} %constant.69.clone.sort_ref, ...), custom_call_target="tpu_custom_call" | custom-call | flops 536870912 | bytes 1048576 | tf_op jit(solution)/shard_map/pallas_call | solution.py:180
  87.6 36.7 %all-to-all-done.2 = bf16[32,256,128]{2,1,0:T(8,128)(2,1)S(1)} async-done(((bf16[32,256,128]{2,1,0:T(8,128)(2,1)}), bf16[32,256,128]{2,1,0:T(8,128)(2,1)S(1)}, u32[]{:S(2)}, u32[]{:S(2)}) %all-to-all-start.2) | async-done | bytes 2097184 | tf_op jit(solution)/shard_map/all_to_all | solution.py:459
  124.3 0.0 copy-start.1
  124.3 1.3 copy-done.1
  125.6 7.0 %shard_map.131 = (bf16[4,2,512,128]{3,2,1,0:T(8,128)(2,1)}, bf16[4,4,512,128]{3,2,1,0:T(8,128)(2,1)}) custom-call(s32[8,2]{1,0:T(8,128)} %copy.20.bounds_ref, bf16[4,8,4,64,128]{4,3,2,1,0:T(8,128)(2,1)} %bitcast.14, bf16[8,512,256]{2,1,0:T(8,128)(2,1)} %projection_ref.5, bf16[2,256,128]{2,1,0:T(8,128)(2,1)} %constant.69.clone.sort_ref, ...), custom_call_target="tpu_custom_call" | custom-call | flops 1073741824 | bytes 2097152 | tf_op jit(solution)/shard_map/pallas_call | solution.py:180
  132.6 1.1 slice.3
  133.7 3.0 %collective-permute-start = (bf16[2,2,512,128]{3,2,1,0:T(8,128)(2,1)S(1)}, bf16[2,2,512,128]{3,2,1,0:T(8,128)(2,1)S(1)}, u32[]{:S(2)}, u32[]{:S(2)}) collective-permute-start(bf16[2,2,512,128]{3,2,1,0:T(8,128)(2,1)S(1)} %slice.3), channel_id=1, source_target_pairs={{1,0},{2,1},{3,2},{4,3},{5,4},{6,5},{7,6},{8,7},{9,8},{10,9},{11,1... | collective-permute-start | bytes 1572872 | tf_op jit(solution)/shard_map/ppermute | solution.py:26
  136.7 12.0 %shard_map.132.rest_3_ = bf16[8,2,8,1024,128]{4,3,2,1,0:T(8,128)(2,1)} custom-call(s32[9]{0:T(128)} %constant.70.clone.plan_ref, f32[256,128]{1,0:T(8,128)} %select_multiply_fusion.turn_ref, bf16[4,4,512,128]{3,2,1,0:T(8,128)(2,1)} %get-tuple-element.19.rest_0_, bf16[4,2,512,128]{3,2,1,0:T(8,128)(2,1)} %get-tuple-element.18.rest_1_), custom_call_target="tpu_custom_call" | custom-call | flops 5368709120 | bytes 10485760 | tf_op jit(solution)/shard_map/pallas_call | solution.py:366
  148.7 10.3 %shard_map.133.rest_4_ = bf16[8,2,8,1024,128]{4,3,2,1,0:T(8,128)(2,1)} custom-call(s32[6]{0:T(128)} %constant.71.clone.plan_ref, f32[256,128]{1,0:T(8,128)} %select_multiply_fusion.turn_ref, bf16[4,4,512,128]{3,2,1,0:T(8,128)(2,1)} %get-tuple-element.19.rest_0_, ...), custom_call_target="tpu_custom_call", output_to_operand_aliasing={{}: (5, {})} | custom-call | flops 4294967296 | bytes 8388608 | tf_op jit(solution)/shard_map/pallas_call | solution.py:366
  159.0 0.0 collective-permute-done.rest_3_
  159.0 0.0 copy-start.3
  159.0 0.8 copy-done.3
  159.8 14.2 %shard_map.134 = bf16[8,2,8,1024,128]{4,3,2,1,0:T(8,128)(2,1)} custom-call(s32[12]{0:T(128)} %constant.72.clone.plan_ref, f32[256,128]{1,0:T(8,128)} %select_multiply_fusion.turn_ref, bf16[2,4,512,128]{3,2,1,0:T(8,128)(2,1)} %get-tuple-element.14.rest_1_.rest_0_, bf16[2,4,512,128]{3,2,1,0:T(8,128)(2,1)} %get-tuple-element.16.rest_1_, ...), custom_call_target="tpu_custom_call", output_to_operand_aliasing={{}: (6, {})} | custom-call | flops 7516192768 | bytes 14680064 | tf_op jit(solution)/shard_map/pallas_call | solution.py:366
  (2 shorter events, 0.0 us)
Async XLA Ops:
  0.0 76.4 %copy-start = (s32[256,2]{0,1:T(2,128)S(1)}, s32[256,2]{0,1:T(2,128)}, u32[]{:S(2)}) copy-start(s32[256,2]{0,1:T(2,128)} %param.15) | copy-start | bytes 6148
  42.0 35.2 %copy-start.5 = (s32[8]{0:T(128)S(1)}, s32[8]{0:T(128)}, u32[]{:S(2)}) copy-start(s32[8]{0:T(128)} %param.16) | copy-start | bytes 100
  42.0 35.3 %copy-start.4 = (s32[256]{0:T(256)S(1)}, s32[256]{0:T(256)}, u32[]{:S(2)}) copy-start(s32[256]{0:T(256)} %constant.67.clone) | copy-start | bytes 3076
  42.0 29.8 %all-to-all-start = ((bf16[32,128,128]{2,1,0:T(8,128)(2,1)}), bf16[32,128,128]{2,1,0:T(8,128)(2,1)S(1)}, u32[]{:S(2)}, u32[]{:S(2)}) async-start(bf16[32,128,128]{2,1,0:T(8,128)(2,1)} %bitcast.18), calls=%async_computation | async-start | bytes 2097152 | tf_op jit(solution)/shard_map/all_to_all | solution.py:459
  71.8 6.8 %copy-start.2 = (bf16[32,128,128]{2,1,0:T(8,128)(2,1)}, bf16[32,128,128]{2,1,0:T(8,128)(2,1)S(1)}, u32[]{:S(2)}) copy-start(bf16[32,128,128]{2,1,0:T(8,128)(2,1)S(1)} %all-to-all-done) | copy-start | bytes 3145732
  71.8 52.5 %all-to-all-start.2 = ((bf16[32,256,128]{2,1,0:T(8,128)(2,1)}), bf16[32,256,128]{2,1,0:T(8,128)(2,1)S(1)}, u32[]{:S(2)}, u32[]{:S(2)}) async-start(bf16[32,256,128]{2,1,0:T(8,128)(2,1)} %bitcast.15), calls=%async_computation.2 | async-start | bytes 4194304 | tf_op jit(solution)/shard_map/all_to_all | solution.py:459
  124.3 1.3 copy-start.1
  133.7 25.3 %collective-permute-start = (bf16[2,2,512,128]{3,2,1,0:T(8,128)(2,1)S(1)}, bf16[2,2,512,128]{3,2,1,0:T(8,128)(2,1)S(1)}, u32[]{:S(2)}, u32[]{:S(2)}) collective-permute-start(bf16[2,2,512,128]{3,2,1,0:T(8,128)(2,1)S(1)} %slice.3), channel_id=1, source_target_pairs={{1,0},{2,1},{3,2},{4,3},{5,4},{6,5},{7,6},{8,7},{9,8},{10,9},{11,1... | collective-permute-start | bytes 1572872 | tf_op jit(solution)/shard_map/ppermute | solution.py:26
  159.0 0.8 copy-start.3

commit v4 on v3

--- a/solution.py
+++ b/solution.py
@@ -17,7 +17,7 @@
 def chunk_sizes(orders):
     if orders < 6:
         return [orders]
-    return [4, 2, 2]
+    return [orders - 3, 2, 1]
 
 
 def shifted(block, axis, distance):
@@ -198,7 +198,7 @@
         scratch_shapes=[
             pltpu.VMEM((groups * degrees // LANES, lat_groups * lanes, LANES), jnp.bfloat16)
         ],
-        compiler_params=pltpu.CompilerParams(vmem_limit_bytes=VMEM_LIMIT),
+        compiler_params=pltpu.CompilerParams(vmem_limit_bytes=16 * 1024 * 1024),
         cost_estimate=pl.CostEstimate(
             flops=2 * wire.size * groups * degrees,
             bytes_accessed=2 * wire.size,
@@ -280,7 +280,7 @@
             if k + 1 < offsets:
                 turn(k + 1, later)
             for i in range(count):
-                left = joined(own, plan_ref[3 * job + 1 + i])
+                left = joined(own, plan_ref[7 * job + 1 + i])
                 product = jnp.dot(left, joined(now), preferred_element_type=jnp.float32)
                 for n in range(tiles // 2):
                     a, b = (
@@ -293,24 +293,24 @@
                     lower = jnp.where(pair, pltpu.roll(a, 6, 1), b)
                     mixed = jnp.stack([upper, lower], axis=1).reshape(2 * tall, LANES)
                     stage[slot, i, k] = mixed.astype(jnp.bfloat16)
+                pltpu.make_async_copy(
+                    stage.at[slot, i, k],
+                    out_ref.at[plan_ref[7 * job + 3 + 2 * i], plan_ref[7 * job + 4 + 2 * i], k],
+                    out_sem.at[slot, i],
+                ).start()
 
     counts = sorted({len(one.places) for one in jobs})
     for count in counts:
         if len(counts) == 1:
             products(count)
         else:
-            pl.when(plan_ref[3 * job] == count)(functools.partial(products, count))
-
-    for n in range(len(jobs)):
-
-        @pl.when(job == n)
-        def _():
+            pl.when(plan_ref[7 * job] == count)(functools.partial(products, count))
+
+    @pl.when(job == len(jobs) - 1)
+    def _():
+        for n in range(max(len(jobs) - 2, 0), len(jobs)):
             for copy in saves(n):
-                copy.start()
-            if n == len(jobs) - 1:
-                for m in range(max(n - 1, 0), n + 1):
-                    for copy in saves(m):
-                        copy.wait()
+                copy.wait()
 
 
 class Job(NamedTuple):
@@ -354,7 +354,12 @@
     jobs = plan_jobs(pairs, spot, own_used, partner_used)
     _, tiles, total, _ = partners[0].shape
     tall = 2 * tiles * LANES
-    plan = [[len(one.places)] + (list(one.buffers) + [0])[:2] for one in jobs]
+    plan = [
+        [len(one.places)]
+        + (list(one.buffers) + [0])[:2]
+        + (list(sum(one.places, ())) + [0, 0])[:4]
+        for one in jobs
+    ]
     operands = [turn] + owns + partners
     specs = [pl.BlockSpec(turn.shape, lambda j, plan_ref: (0, 0))]
     specs += [pl.BlockSpec(memory_space=pl.ANY)] * len(owns + partners)
@@ -385,7 +390,7 @@
         ),
         out_shape=shape,
         input_output_aliases=aliases,
-        compiler_params=pltpu.CompilerParams(vmem_limit_bytes=VMEM_LIMIT),
+        compiler_params=pltpu.CompilerParams(vmem_limit_bytes=44 * 1024 * 1024),
         cost_estimate=pl.CostEstimate(
             flops=2 * len(pairs) * offsets * total * tall * tiles * LANES,
             bytes_accessed=2 * len(pairs) * offsets * tall * tiles * LANES,
@@ -427,7 +432,7 @@
     grouped = frames.reshape(groups, times, lat_rows, lon_count)
     sent = list(azimuthal_transform(tables[:1], grouped, steps))
     if len(sizes) > 1:
-        sent += list(azimuthal_transform(tables[1:], grouped, steps))
+        sent += list(azimuthal_transform(tables[1:], grouped, min(4, times)))
 
     rank = lax.axis_index("tm") * lat_groups + lax.axis_index("lat")
     bounds = lax.dynamic_slice_in_dim(degree_range, rank * orders, orders, 0)

time: 176 us -> 169 us (0.960)
  waiting for transfers between devices: 54.5 us -> 67.9 us
  blocking collectives: 31.7 us -> 20.6 us
  Pallas kernels: 70.1 us -> 61.6 us
    all_to_all x2, waiting for transfers between devices: 54.5 us -> 67.9 us  [shards(): lax.all_to_all(packed, ('tm', 'lat'), split_axis=0, concat_axis=0, tiled=...]
    all_to_all x1, blocking collectives: 31.7 us -> 20.6 us  [shards(): lax.all_to_all(packed, ('tm', 'lat'), split_axis=0, concat_axis=0, tiled=...]
    pallas_call x3, Pallas kernels: 36.5 us -> 31.8 us  [couple(): pl.pallas_call(functools.partial(couple_kernel, jobs, len(owns), len(part...]
    pallas_call x3, Pallas kernels: 16 us -> 11.7 us  [legendre(): pl.pallas_call(functools.partial(legendre_kernel, groups, first), grid=(o...]
    unnamed x13 -> x35, local copies, waits for them, and re-layouts: 2.79 us -> 3.6 us
  transfers between devices with their start and end apart: 3 -> 3, of which waited for: 2 -> 2; matrix products, arithmetic and copies ran while one was open for 1% -> 1% of each run, Pallas kernels for 22% -> 16%
where the time goes in v4:
time: 169 us; the launch traced here: 167 us
  waiting for transfers between devices  67.9 us (40%)
  Pallas kernels  61.6 us (36%)
  blocking collectives  20.6 us (12%)
  starting transfers between devices  12.1 us (7%)
  local copies, waits for them, and re-layouts  3.86 us (2%)
    all_to_all x2, waiting for transfers between devices, shards(): lax.all_to_all(packed, ('tm', 'lat'), split_axis=0, concat_axis=0, tiled=...  67.9 us
    pallas_call x3, Pallas kernels, couple(): pl.pallas_call(functools.partial(couple_kernel, jobs, len(owns), len(part...  31.8 us
    all_to_all x1, blocking collectives, shards(): lax.all_to_all(packed, ('tm', 'lat'), split_axis=0, concat_axis=0, tiled=...  20.6 us
    pallas_call x2, Pallas kernels, azimuthal_transform(): pl.pallas_call(functools.partial(azimuthal_kernel, steps, count), in_spec...  18.1 us
    pallas_call x3, Pallas kernels, legendre(): pl.pallas_call(functools.partial(legendre_kernel, groups, first), grid=(o...  11.7 us
    all_to_all x2, starting transfers between devices, shards(): lax.all_to_all(packed, ('tm', 'lat'), split_axis=0, concat_axis=0, tiled=...  9.02 us
    unnamed x35, local copies, waits for them, and re-layouts  3.6 us
  transfers between devices with their start and end apart: 3, of which 2 were waited for; matrix products, arithmetic and copies ran while one was open for 1% of the time, Pallas kernels for 16%

profile of v4, /device:TPU:7, one launch (start us, length us, event | category | flops | bytes accessed | tf_op | source)
XLA Modules:
  0.0 167.1 jit_solution(9549933728190164972)
XLA Ops:
  0.0 0.0 copy-start
  0.0 10.0 %shard_map.127 = (bf16[64,32,2,128]{3,2,1,0:T(2,128)(2,1)}, bf16[32,32,2,128]{3,2,1,0:T(2,128)(2,1)}) custom-call(bf16[128,1024]{1,0:T(8,128)(2,1)} %constant.76.refs_0_, bf16[64,1024]{1,0:T(8,128)(2,1)} %constant.77.refs_1_, bf16[2,32,64,1024]{3,2,1,0:T(8,128)(2,1)} %bitcast.14), custom_call_target="tpu_custom_call" | custom-call | flops 1610612736 | bytes 8388608 | tf_op jit(solution)/shard_map/pallas_call | solution.py:89
  10.0 20.6 %all_to_all.15 = bf16[32,64,128]{2,1,0:T(8,128)(2,1)S(1)} all-to-all(bf16[32,64,128]{2,1,0:T(8,128)(2,1)} %bitcast.18), channel_id=1, replica_groups=mesh['tm'=4,'lat'=8] {'tm','lat'}, dimensions={0} | all-to-all | bytes 1048576 | tf_op jit(solution)/shard_map/all_to_all | solution.py:464
  30.5 4.4 %all-to-all-start = ((bf16[32,128,128]{2,1,0:T(8,128)(2,1)}), bf16[32,128,128]{2,1,0:T(8,128)(2,1)S(1)}, u32[]{:S(2)}, u32[]{:S(2)}) async-start(bf16[32,128,128]{2,1,0:T(8,128)(2,1)} %bitcast.17), calls=%async_computation | async-start | bytes 2097152 | tf_op jit(solution)/shard_map/all_to_all | solution.py:464
  34.9 8.2 %shard_map.130 = bf16[160,32,2,128]{3,2,1,0:T(2,128)(2,1)} custom-call(bf16[320,1024]{1,0:T(8,128)(2,1)} %constant.78.refs_0_, bf16[2,32,64,1024]{3,2,1,0:T(8,128)(2,1)} %bitcast.15), custom_call_target="tpu_custom_call" | custom-call | flops 2684354560 | bytes 8388608 | tf_op jit(solution)/shard_map/pallas_call | solution.py:89
  43.1 17.1 %all-to-all-done = bf16[32,128,128]{2,1,0:T(8,128)(2,1)S(1)} async-done(((bf16[32,128,128]{2,1,0:T(8,128)(2,1)}), bf16[32,128,128]{2,1,0:T(8,128)(2,1)S(1)}, u32[]{:S(2)}, u32[]{:S(2)}) %all-to-all-start) | async-done | bytes 1048608 | tf_op jit(solution)/shard_map/all_to_all | solution.py:464
  60.2 0.0 copy-start.5
  60.2 1.0 copy-done.5
  61.2 0.0 copy-start.16
  61.2 0.0 copy-start.15
  61.2 0.0 copy-start.1
  61.2 0.0 copy-start.2
  61.2 0.0 copy-start.7
  61.2 4.6 %all-to-all-start.2 = ((bf16[32,320,128]{2,1,0:T(8,128)(2,1)}), bf16[32,320,128]{2,1,0:T(8,128)(2,1)}, u32[]{:S(2)}, u32[]{:S(2)}) async-start(bf16[32,320,128]{2,1,0:T(8,128)(2,1)} %bitcast.16), calls=%async_computation.2 | async-start | bytes 5242880 | tf_op jit(solution)/shard_map/all_to_all | solution.py:464
  65.8 0.0 copy-done
  65.8 0.1 constant_dynamic-slice_fusion
  65.9 0.1 copy.20.bounds_ref
  66.0 0.0 copy-done.16
  66.0 0.1 broadcast_in_dim.15
  66.1 0.1 reshape.49
  66.2 0.0 copy-start.6
  66.2 0.0 copy-done.15
  66.2 0.6 select_multiply_fusion.turn_ref
  66.8 0.0 copy-done.1
  66.8 0.0 copy-done.2
  66.8 0.0 copy-done.7
  66.8 1.8 %shard_map.129 = (bf16[1,2,512,128]{3,2,1,0:T(8,128)(2,1)S(1)}, bf16[1,4,512,128]{3,2,1,0:T(8,128)(2,1)S(1)}) custom-call(s32[8,2]{1,0:T(8,128)S(1)} %copy.20.bounds_ref, bf16[4,8,1,64,128]{4,3,2,1,0:T(8,128)(2,1)S(1)} %bitcast.13, bf16[8,512,256]{2,1,0:T(8,128)(2,1)S(1)} %copy-done.1, bf16[2,256,128]{2,1,0:T(8,128)(2,1)S(1)} %copy-done.7, ...), custom_call_target="tpu_custom_call" | custom-call | flops 268435456 | bytes 524288 | tf_op jit(solution)/shard_map/pallas_call | solution.py:180
  68.7 0.0 copy-start.8
  68.7 0.8 copy-done.8
  69.4 0.0 copy-start.10
  69.5 0.7 copy-done.10
  70.2 0.0 copy-done.6
  70.2 3.0 %shard_map.128 = (bf16[2,2,512,128]{3,2,1,0:T(8,128)(2,1)S(1)}, bf16[2,4,512,128]{3,2,1,0:T(8,128)(2,1)S(1)}) custom-call(s32[8,2]{1,0:T(8,128)S(1)} %copy.20.bounds_ref, bf16[4,8,2,64,128]{4,3,2,1,0:T(8,128)(2,1)S(1)} %bitcast.12, bf16[8,512,256]{2,1,0:T(8,128)(2,1)S(1)} %copy-done.1, bf16[2,256,128]{2,1,0:T(8,128)(2,1)S(1)} %copy-done.7, ...), custom_call_target="tpu_custom_call" | custom-call | flops 536870912 | bytes 1048576 | tf_op jit(solution)/shard_map/pallas_call | solution.py:180
  73.2 0.0 copy-start.3
  73.2 1.0 copy-done.3
  74.2 50.8 %all-to-all-done.2 = bf16[32,320,128]{2,1,0:T(8,128)(2,1)} async-done(((bf16[32,320,128]{2,1,0:T(8,128)(2,1)}), bf16[32,320,128]{2,1,0:T(8,128)(2,1)}, u32[]{:S(2)}, u32[]{:S(2)}) %all-to-all-start.2) | async-done | bytes 2621472 | tf_op jit(solution)/shard_map/all_to_all | solution.py:464
  125.0 0.0 copy-start.12
  125.0 6.8 %shard_map.131 = (bf16[5,2,512,128]{3,2,1,0:T(8,128)(2,1)S(1)}, bf16[5,4,512,128]{3,2,1,0:T(8,128)(2,1)S(1)}) custom-call(s32[8,2]{1,0:T(8,128)S(1)} %copy.20.bounds_ref, bf16[4,8,5,64,128]{4,3,2,1,0:T(8,128)(2,1)} %bitcast.6.wire_ref, bf16[8,512,256]{2,1,0:T(8,128)(2,1)S(1)} %copy-done.1, bf16[2,256,128]{2,1,0:T(8,128)(2,1)S(1)} %copy-done.7, ...), custom_call_target="tpu_custom_call" | custom-call | flops 1342177280 | bytes 2621440 | tf_op jit(solution)/shard_map/pallas_call | solution.py:180
  131.9 3.1 %collective-permute-start = (bf16[2,2,512,128]{3,2,1,0:T(8,128)(2,1)S(1)}, bf16[2,2,512,128]{3,2,1,0:T(8,128)(2,1)S(1)}, u32[]{:S(2)}, u32[]{:S(2)}) collective-permute-start(bf16[2,2,512,128]{3,2,1,0:T(8,128)(2,1)S(1)} %slice.3), channel_id=1, source_target_pairs={{1,0},{2,1},{3,2},{4,3},{5,4},{6,5},{7,6},{8,7},{9,8},{10,9},{11,1... | collective-permute-start | bytes 1572872 | tf_op jit(solution)/shard_map/ppermute | solution.py:26
  135.0 0.0 copy-done.12
  135.0 0.0 copy-start.4
  135.0 0.0 copy-start.14
  135.0 12.9 %shard_map.132.rest_4_ = bf16[8,2,8,1024,128]{4,3,2,1,0:T(8,128)(2,1)} custom-call(s32[28]{0:T(128)S(1)} %copy-done.12, f32[256,128]{1,0:T(8,128)S(1)} %select_multiply_fusion.turn_ref, bf16[5,4,512,128]{3,2,1,0:T(8,128)(2,1)S(1)} %get-tuple-element.19.rest_0_, bf16[5,2,512,128]{3,2,1,0:T(8,128)(2,1)S(1)} %get-tuple-element.18.rest_1_), custom_call_target="tpu_custom_call" | custom-call | flops 7516192768 | bytes 14680064 | tf_op jit(solution)/shard_map/pallas_call | solution.py:371
  147.9 0.0 collective-permute-done.rest_3_
  147.9 0.0 copy-done.4
  148.0 0.0 copy-done.14
  148.0 0.0 copy-start.9
  148.0 0.0 copy-start.11
  148.0 0.0 copy-start.13
  148.0 9.9 %shard_map.133.rest_4_ = bf16[8,2,8,1024,128]{4,3,2,1,0:T(8,128)(2,1)} custom-call(s32[21]{0:T(128)S(1)} %copy-done.14, f32[256,128]{1,0:T(8,128)S(1)} %select_multiply_fusion.turn_ref, bf16[5,4,512,128]{3,2,1,0:T(8,128)(2,1)S(1)} %get-tuple-element.19.rest_0_, bf16[2,4,512,128]{3,2,1,0:T(8,128)(2,1)S(1)} %copy-done.4, ...), custom_call_target="tpu_custom_call", output_to_operand_aliasing={{}: (6, {})} | custom-call | flops 5368709120 | bytes 10485760 | tf_op jit(solution)/shard_map/pallas_call | solution.py:371
  157.9 0.0 copy-done.9
  158.0 0.0 copy-done.11
  158.0 0.0 copy-done.13
  158.0 9.0 %shard_map.134 = bf16[8,2,8,1024,128]{4,3,2,1,0:T(8,128)(2,1)} custom-call(s32[21]{0:T(128)S(1)} %copy-done.13, f32[256,128]{1,0:T(8,128)S(1)} %select_multiply_fusion.turn_ref, bf16[2,4,512,128]{3,2,1,0:T(8,128)(2,1)S(1)} %copy-done.4, bf16[1,4,512,128]{3,2,1,0:T(8,128)(2,1)S(1)} %copy-done.9, ...), custom_call_target="tpu_custom_call", output_to_operand_aliasing={{}: (6, {})} | custom-call | flops 4294967296 | bytes 8388608 | tf_op jit(solution)/shard_map/pallas_call | solution.py:371
  (3 shorter events, 0.0 us)
Async XLA Ops:
  0.0 65.8 %copy-start = (s32[256,2]{0,1:T(2,128)S(1)}, s32[256,2]{0,1:T(2,128)}, u32[]{:S(2)}) copy-start(s32[256,2]{0,1:T(2,128)} %param.15) | copy-start | bytes 6148
  30.5 29.7 %all-to-all-start = ((bf16[32,128,128]{2,1,0:T(8,128)(2,1)}), bf16[32,128,128]{2,1,0:T(8,128)(2,1)S(1)}, u32[]{:S(2)}, u32[]{:S(2)}) async-start(bf16[32,128,128]{2,1,0:T(8,128)(2,1)} %bitcast.17), calls=%async_computation | async-start | bytes 2097152 | tf_op jit(solution)/shard_map/all_to_all | solution.py:464
  60.2 1.0 copy-start.5
  61.2 4.8 %copy-start.16 = (s32[8]{0:T(128)S(1)}, s32[8]{0:T(128)}, u32[]{:S(2)}) copy-start(s32[8]{0:T(128)} %param.16) | copy-start | bytes 100
  61.2 5.0 %copy-start.15 = (s32[256]{0:T(256)S(1)}, s32[256]{0:T(256)}, u32[]{:S(2)}) copy-start(s32[256]{0:T(256)} %constant.67.clone) | copy-start | bytes 3076
  61.2 5.6 %copy-start.1 = (bf16[8,512,256]{2,1,0:T(8,128)(2,1)S(1)}, bf16[8,512,256]{2,1,0:T(8,128)(2,1)}, u32[]{:S(2)}) copy-start(bf16[8,512,256]{2,1,0:T(8,128)(2,1)} %projection_ref.5) | copy-start | bytes 6291460
  61.2 5.6 %copy-start.2 = (bf16[4,512,128]{2,1,0:T(8,128)(2,1)S(1)}, bf16[4,512,128]{2,1,0:T(8,128)(2,1)}, u32[]{:S(2)}) copy-start(bf16[4,512,128]{2,1,0:T(8,128)(2,1)} %constant.68.clone.twice_ref) | copy-start | bytes 1572868
  61.2 5.6 %copy-start.7 = (bf16[2,256,128]{2,1,0:T(8,128)(2,1)S(1)}, bf16[2,256,128]{2,1,0:T(8,128)(2,1)}, u32[]{:S(2)}) copy-start(bf16[2,256,128]{2,1,0:T(8,128)(2,1)} %constant.69.clone.sort_ref) | copy-start | bytes 393220
  61.2 63.8 %all-to-all-start.2 = ((bf16[32,320,128]{2,1,0:T(8,128)(2,1)}), bf16[32,320,128]{2,1,0:T(8,128)(2,1)}, u32[]{:S(2)}, u32[]{:S(2)}) async-start(bf16[32,320,128]{2,1,0:T(8,128)(2,1)} %bitcast.16), calls=%async_computation.2 | async-start | bytes 5242880 | tf_op jit(solution)/shard_map/all_to_all | solution.py:464
  66.2 4.0 %copy-start.6 = (bf16[32,128,128]{2,1,0:T(8,128)(2,1)S(1)}, bf16[32,128,128]{2,1,0:T(8,128)(2,1)}, u32[]{:S(2)}) copy-start(bf16[32,128,128]{2,1,0:T(8,128)(2,1)} %copy-done.5) | copy-start | bytes 3145732
  68.7 0.8 copy-start.8
  69.4 0.7 copy-start.10
  73.2 1.0 copy-start.3
  125.0 10.0 %copy-start.12 = (s32[28]{0:T(128)S(1)}, s32[28]{0:T(128)}, u32[]{:S(2)}) copy-start(s32[28]{0:T(128)} %constant.70.clone.plan_ref) | copy-start | bytes 340
  131.9 16.0 %collective-permute-start = (bf16[2,2,512,128]{3,2,1,0:T(8,128)(2,1)S(1)}, bf16[2,2,512,128]{3,2,1,0:T(8,128)(2,1)S(1)}, u32[]{:S(2)}, u32[]{:S(2)}) collective-permute-start(bf16[2,2,512,128]{3,2,1,0:T(8,128)(2,1)S(1)} %slice.3), channel_id=1, source_target_pairs={{1,0},{2,1},{3,2},{4,3},{5,4},{6,5},{7,6},{8,7},{9,8},{10,9},{11,1... | collective-permute-start | bytes 1572872 | tf_op jit(solution)/shard_map/ppermute | solution.py:26
  135.0 13.0 %copy-start.4 = (bf16[2,4,512,128]{3,2,1,0:T(8,128)(2,1)S(1)}, bf16[2,4,512,128]{3,2,1,0:T(8,128)(2,1)}, u32[]{:S(2)}) copy-start(bf16[2,4,512,128]{3,2,1,0:T(8,128)(2,1)} %copy-done.3) | copy-start | bytes 3145732
  135.0 13.0 %copy-start.14 = (s32[21]{0:T(128)S(1)}, s32[21]{0:T(128)}, u32[]{:S(2)}) copy-start(s32[21]{0:T(128)} %constant.71.clone.plan_ref) | copy-start | bytes 256
  148.0 10.0 %copy-start.9 = (bf16[1,4,512,128]{3,2,1,0:T(8,128)(2,1)S(1)}, bf16[1,4,512,128]{3,2,1,0:T(8,128)(2,1)}, u32[]{:S(2)}) copy-start(bf16[1,4,512,128]{3,2,1,0:T(8,128)(2,1)} %copy-done.8) | copy-start | bytes 1572868
  148.0 10.0 %copy-start.11 = (bf16[1,2,512,128]{3,2,1,0:T(8,128)(2,1)S(1)}, bf16[1,2,512,128]{3,2,1,0:T(8,128)(2,1)}, u32[]{:S(2)}) copy-start(bf16[1,2,512,128]{3,2,1,0:T(8,128)(2,1)} %copy-done.10) | copy-start | bytes 786436
  148.0 10.0 %copy-start.13 = (s32[21]{0:T(128)S(1)}, s32[21]{0:T(128)}, u32[]{:S(2)}) copy-start(s32[21]{0:T(128)} %constant.72.clone.plan_ref) | copy-start | bytes 256
